TPU v7x, 32 devices: a whole 2x2x4 slice. The times are simulated.
32 devices in a mesh: rows: 4 (over y, x), seq: 8 (over z, core).
Axes of the slice: x: 2, y: 2, z: 4, core: 2. Of those that a mesh axis runs over, the one named last changes fastest.
Arguments:
- residual_in: float32 [32, 1024, 512], P('rows', 'seq'), may hold values from -6 to 6
- cotangent: float32 [32, 1024, 512], P('rows', 'seq'), may hold values from -6 to 6
- segments: int32 [32, 1024], P('rows'), may hold values from 0 to 7, never falling along the last dimension, each value on 1 to 512 neighbouring positions
- owners: int32 [96], replicated, may hold values from 0 to 7, as said below
- master_tiles: float32 [128, 512, 128], P('seq'), may hold values from -0.53033009 to 0.53033009, as said below
- first_tiles: float32 [128, 512, 128], P('seq'), may hold values from -0.0024414062 to 0.0024414062
- second_tiles: float32 [128, 512, 128], P('seq'), may hold values from 1.5873903e-07 to 6.349561e-07
- norm_params: float32 [8, 512], replicated, may hold values from -2 to 2
- norm_first: float32 [8, 512], replicated, may hold values from -0.009765625 to 0.009765625
- norm_second: float32 [8, 512], replicated, may hold values from 2.5398244e-06 to 1.0159298e-05
Outputs:
- residual_out: float32 [32, 1024, 512], P('rows', 'seq')
- input_grad: float32 [32, 1024, 512], P('rows', 'seq')
- tile_grads: float32 [128, 512, 128], P('seq')
- grad_norm: float32 [1], replicated
- new_first: float32 [128, 512, 128], P('seq')
- new_second: float32 [128, 512, 128], P('seq')
- new_master: float32 [128, 512, 128], P('seq')
- new_copies: bfloat16 [128, 512, 128], P('seq')
- norm_grads: float32 [8, 512], replicated
- new_norm_first: float32 [8, 512], replicated
- new_norm_second: float32 [8, 512], replicated
- new_norm_params: float32 [8, 512], replicated
Inputs may be any that keep to these rules, and one draw needn't show every extreme that they name: `owners`: no device owns more than 16 tiles, and one device owns exactly 16. `segments`: along a row the document numbers never fall; a document has 1 to 512 positions and some document exactly 512. `master_tiles`: slot 16 d + n holds the tile with the n-th smallest number among those owned by device d; slots that hold no tile are ignored.
All inputs are finite; a program needn't handle non-finite values.
Results may differ from a plain program's by a relative error of at most 0.013.
Values may be sent and summed in bfloat16 or wider, within the bound.
A program may use at most 256 MiB of HBM per device.

v0:
```python
import jax
import jax.numpy as jnp
from jax import lax
from jax.experimental import pallas as pl
from jax.experimental.pallas import tpu as pltpu

from jax.sharding import PartitionSpec as P

HEADS = 8
LAYERS = 2
STEP = 5


def norm_layer(values, gain, offset):
    center = values - jnp.mean(values, axis=-1, keepdims=True)
    spread = jnp.mean(center * center, axis=-1, keepdims=True)
    return center * lax.rsqrt(spread + 1e-05) * gain + offset


def matmul(left, right):
    return jnp.dot(left, right, preferred_element_type=jnp.float32)


def left_product(left, right):
    return lax.dot_general(
        left, right, (((0,), (0,)), ((), ())), preferred_element_type=jnp.float32
    )


def right_product(left, right):
    return lax.dot_general(
        left, right, (((1,), (1,)), ((), ())), preferred_element_type=jnp.float32
    )


def assemble(weight_tiles, layer_number):
    first_tile = 48 * layer_number
    model_width = weight_tiles.shape[1]
    qkv_weight = (
        weight_tiles[first_tile : first_tile + 12].transpose(1, 0, 2).reshape(model_width, -1)
    )
    out_weight = (
        weight_tiles[first_tile + 12 : first_tile + 16].transpose(1, 0, 2).reshape(model_width, -1)
    )
    up_weight = (
        weight_tiles[first_tile + 16 : first_tile + 32].transpose(1, 0, 2).reshape(model_width, -1)
    )
    down_block = weight_tiles[first_tile + 32 : first_tile + 48].reshape(4, 4, model_width, -1)
    down_weight = down_block.transpose(0, 2, 1, 3).reshape(4 * model_width, model_width)
    return (qkv_weight, out_weight, up_weight, down_weight)


def split_tiles(qkv_grad, out_grad, up_grad, down_grad, tile_width):
    model_width = qkv_grad.shape[0]
    pieces = [
        qkv_grad.reshape(model_width, -1, tile_width).transpose(1, 0, 2),
        out_grad.reshape(model_width, -1, tile_width).transpose(1, 0, 2),
        up_grad.reshape(model_width, -1, tile_width).transpose(1, 0, 2),
        down_grad.reshape(4, model_width, 4, tile_width)
        .transpose(0, 2, 1, 3)
        .reshape(16, model_width, tile_width),
    ]
    return jnp.concatenate(pieces, axis=0)


def attend_forward(queries, key_rows, value_rows, doc_ids, block_rows, scale):
    length = queries.shape[0]

    def one_block(number):
        first_row = number * block_rows
        query_block = lax.dynamic_slice_in_dim(queries, first_row, block_rows, 0)
        doc_block = lax.dynamic_slice_in_dim(doc_ids, first_row, block_rows, 0)
        same_doc = doc_block[:, None] == doc_ids[None, :]
        scores = jnp.where(same_doc, right_product(query_block, key_rows) * scale, -1e30)
        largest = jnp.max(scores, axis=-1, keepdims=True)
        row_total = jnp.sum(jnp.exp(scores - largest), axis=-1, keepdims=True)
        logsum = largest + jnp.log(row_total)
        weights = jnp.where(same_doc, jnp.exp(scores - logsum), 0.0).astype(jnp.bfloat16)
        return (matmul(weights, value_rows).astype(jnp.bfloat16), logsum[:, 0])

    outputs, logsums = lax.map(one_block, jnp.arange(length // block_rows))
    return (outputs.reshape(length, -1), logsums.reshape(length))


def attend_backward(queries, key_rows, value_rows, doc_ids, logsums, out_grads, block_rows, scale):
    length, head_dim = queries.shape

    def one_block(carry, number):
        key_grad, value_grad = carry
        first_row = number * block_rows
        query_block = lax.dynamic_slice_in_dim(queries, first_row, block_rows, 0)
        doc_block = lax.dynamic_slice_in_dim(doc_ids, first_row, block_rows, 0)
        logsum_block = lax.dynamic_slice_in_dim(logsums, first_row, block_rows, 0)
        grad_block = lax.dynamic_slice_in_dim(out_grads, first_row, block_rows, 0)
        same_doc = doc_block[:, None] == doc_ids[None, :]
        scores = jnp.where(same_doc, right_product(query_block, key_rows) * scale, -1e30)
        probs = jnp.where(same_doc, jnp.exp(scores - logsum_block[:, None]), 0.0)
        prob_grad = right_product(grad_block, value_rows)
        inner_sum = jnp.sum(probs * prob_grad, axis=-1, keepdims=True)
        score_grad = (probs * (prob_grad - inner_sum)).astype(jnp.bfloat16)
        query_grad = matmul(score_grad, key_rows) * scale
        key_grad = key_grad + left_product(score_grad, query_block) * scale
        value_grad = value_grad + left_product(probs.astype(jnp.bfloat16), grad_block)
        return ((key_grad, value_grad), query_grad)

    zeros_block = jnp.zeros((length, head_dim), jnp.float32)
    (key_grad, value_grad), query_grads = lax.scan(
        one_block, (zeros_block, zeros_block), jnp.arange(length // block_rows)
    )
    stacked = jnp.stack([query_grads.reshape(length, head_dim), key_grad, value_grad], axis=1)
    return stacked.astype(jnp.bfloat16)


def adamw(weight, grad, first, second, learn_rate, correction):
    first = 0.5 * first + 0.5 * grad
    second = 0.5 * second + 0.5 * grad * grad
    update = first / correction / (jnp.sqrt(second / correction) + 1e-08)
    return (weight - learn_rate * (update + 0.01 * weight), first, second)


def local_by_heads(
    residual_in,
    cotangent,
    segments,
    owners,
    master_tiles,
    first_tiles,
    second_tiles,
    norm_params,
    norm_first,
    norm_second,
):
    local_rows, positions, model_width = residual_in.shape
    seq_devices = lax.axis_size("seq")
    seq_index = lax.axis_index("seq")
    head_dim = model_width // HEADS
    group_count = seq_devices // HEADS
    group_rows = local_rows // group_count
    length = positions * seq_devices
    block_rows = min(512, length)
    scale = head_dim ** (-0.5)
    tile_total = owners.shape[0]
    capacity = master_tiles.shape[0]
    tile_width = master_tiles.shape[2]
    places = jnp.arange(tile_total, dtype=jnp.int32)
    before = (owners[None, :] == owners[:, None]) & (places[None, :] < places[:, None])
    ranks = jnp.sum(before.astype(jnp.int32), axis=1)
    slot_ids = owners * capacity + ranks
    local_slots = jnp.arange(capacity, dtype=jnp.int32)
    matches = (owners[:, None] == seq_index) & (ranks[:, None] == local_slots[None, :])
    chosen = jnp.sum(jnp.where(matches, places[:, None], 0), axis=0)
    present = jnp.any(matches, axis=0)
    copies = lax.all_gather(master_tiles.astype(jnp.bfloat16), "seq", axis=0, tiled=True)
    weight_tiles = jnp.take(copies, slot_ids, axis=0)
    my_group = seq_index // HEADS
    doc_rows = lax.dynamic_slice_in_dim(segments, my_group * group_rows, group_rows, 0)
    hidden = residual_in.reshape(-1, model_width)
    saved = []
    for layer_number in range(LAYERS):
        qkv_weight, out_weight, up_weight, down_weight = assemble(weight_tiles, layer_number)
        params = norm_params[4 * layer_number : 4 * layer_number + 4]
        normed, first_pull = jax.vjp(norm_layer, hidden, params[0], params[1])
        normed_low = normed.astype(jnp.bfloat16)
        packed = matmul(normed_low, qkv_weight).astype(jnp.bfloat16)
        outgoing = packed.reshape(group_count, group_rows, positions, 3, HEADS, head_dim)
        outgoing = outgoing.transpose(0, 4, 1, 2, 3, 5).reshape(
            seq_devices, group_rows, positions * 3 * head_dim
        )
        arrived = lax.all_to_all(outgoing, "seq", split_axis=0, concat_axis=2, tiled=True).reshape(
            group_rows, length, 3, head_dim
        )

        def forward_item(items):
            return attend_forward(
                items[0][:, 0], items[0][:, 1], items[0][:, 2], items[1], block_rows, scale
            )

        attended, logsums = lax.map(forward_item, (arrived, doc_rows))
        returning = attended.reshape(1, group_rows, seq_devices, positions * head_dim)
        mixed = lax.all_to_all(returning, "seq", split_axis=2, concat_axis=0, tiled=True)
        mixed = (
            mixed.reshape(group_count, HEADS, group_rows, positions, head_dim)
            .transpose(0, 2, 3, 1, 4)
            .reshape(-1, model_width)
        )
        middle = hidden + matmul(mixed, out_weight)
        normed_two, second_pull = jax.vjp(norm_layer, middle, params[2], params[3])
        normed_two_low = normed_two.astype(jnp.bfloat16)
        inner = matmul(normed_two_low, up_weight)
        active = jax.nn.gelu(inner).astype(jnp.bfloat16)
        hidden = middle + matmul(active, down_weight)
        saved.append(
            (
                first_pull,
                normed_low,
                arrived,
                logsums,
                mixed,
                second_pull,
                normed_two_low,
                inner,
                active,
            )
        )
    grad = cotangent.reshape(-1, model_width)
    tile_parts = [None] * LAYERS
    norm_parts = [None] * LAYERS
    for layer_number in reversed(range(LAYERS)):
        (
            first_pull,
            normed_low,
            arrived,
            logsums,
            mixed,
            second_pull,
            normed_two_low,
            inner,
            active,
        ) = saved[layer_number]
        qkv_weight, out_weight, up_weight, down_weight = assemble(weight_tiles, layer_number)
        grad_low = grad.astype(jnp.bfloat16)
        down_grad = left_product(active, grad_low)
        active_grad = right_product(grad_low, down_weight)
        inner_grad = jax.vjp(jax.nn.gelu, inner)[1](active_grad)[0].astype(jnp.bfloat16)
        up_grad = left_product(normed_two_low, inner_grad)
        middle_part, gain_two, offset_two = second_pull(right_product(inner_grad, up_weight))
        middle_grad = grad + middle_part
        middle_low = middle_grad.astype(jnp.bfloat16)
        out_grad = left_product(mixed, middle_low)
        mixed_grad = right_product(middle_low, out_weight).astype(jnp.bfloat16)
        sending = mixed_grad.reshape(group_count, group_rows, positions, HEADS, head_dim)
        sending = sending.transpose(0, 3, 1, 2, 4).reshape(
            seq_devices, group_rows, positions * head_dim
        )
        head_grads = lax.all_to_all(
            sending, "seq", split_axis=0, concat_axis=2, tiled=True
        ).reshape(group_rows, length, head_dim)

        def backward_item(items):
            arrived_row, doc_row, logsum_row, grad_row = items
            return attend_backward(
                arrived_row[:, 0],
                arrived_row[:, 1],
                arrived_row[:, 2],
                doc_row,
                logsum_row,
                grad_row,
                block_rows,
                scale,
            )

        packed_grads = lax.map(backward_item, (arrived, doc_rows, logsums, head_grads))
        coming = lax.all_to_all(
            packed_grads.reshape(1, group_rows, seq_devices, positions * 3 * head_dim),
            "seq",
            split_axis=2,
            concat_axis=0,
            tiled=True,
        )
        qkv_grad = coming.reshape(group_count, HEADS, group_rows, positions, 3, head_dim)
        qkv_grad = qkv_grad.transpose(0, 2, 3, 4, 1, 5).reshape(-1, 3 * model_width)
        qkv_weight_grad = left_product(normed_low, qkv_grad)
        input_part, gain_one, offset_one = first_pull(right_product(qkv_grad, qkv_weight))
        grad = middle_grad + input_part
        tile_parts[layer_number] = split_tiles(
            qkv_weight_grad, out_grad, up_grad, down_grad, tile_width
        )
        norm_parts[layer_number] = jnp.stack([gain_one, offset_one, gain_two, offset_two])
    dense = jnp.concatenate(tile_parts, axis=0)
    norm_part = jnp.concatenate(norm_parts, axis=0)
    piece = lax.psum_scatter(
        dense.reshape(-1, tile_width), ("rows", "seq"), scatter_dimension=0, tiled=True
    )
    squares, norm_sum = lax.psum((jnp.sum(piece * piece), norm_part), ("rows", "seq"))
    summed = (
        lax.all_gather(piece.astype(jnp.bfloat16), ("rows", "seq"), axis=0, tiled=True)
        .astype(piece.dtype)
        .reshape(dense.shape)
    )
    owned = jnp.take(summed, chosen, axis=0)
    keep = present[:, None, None]
    owned = jnp.where(keep, owned, 0.0)
    total = jnp.sqrt(squares + jnp.sum(norm_sum * norm_sum))
    factor = 1.0 / jnp.maximum(total, 1.0)
    clipped = owned * factor
    norm_clip = norm_sum * factor
    correction = 1.0 - 0.5**STEP
    new_weight, new_first_rows, new_second_rows = adamw(
        master_tiles, clipped, first_tiles, second_tiles, 0.05, correction
    )
    new_weight = jnp.where(keep, new_weight, 0.0)
    new_first_rows = jnp.where(keep, new_first_rows, 0.0)
    new_second_rows = jnp.where(keep, new_second_rows, 0.0)
    new_norm, new_norm_f, new_norm_s = adamw(
        norm_params, norm_clip, norm_first, norm_second, 0.25, correction
    )
    return (
        hidden.reshape(local_rows, positions, model_width),
        grad.reshape(local_rows, positions, model_width),
        clipped,
        total[None],
        new_first_rows,
        new_second_rows,
        new_weight,
        new_weight.astype(jnp.bfloat16),
        norm_clip,
        new_norm_f,
        new_norm_s,
        new_norm,
    )


F32 = jnp.float32
BF16 = jnp.bfloat16
BLOCK = 256
DENSE = 512
DENSE_BACK = 512
QUERY = 128
UNROLL = 4
UNROLL_BACK = 4
VMEM_BYTES = 60 * 1024 * 1024


def dot_nn(left, right):
    return jnp.dot(left, right, preferred_element_type=F32)


def dot_nt(left, right, precision=None):
    return lax.dot_general(
        left, right, (((1,), (1,)), ((), ())), preferred_element_type=F32, precision=precision
    )


def dot_tn(left, right):
    return lax.dot_general(left, right, (((0,), (0,)), ((), ())), preferred_element_type=F32)


def rows_of(number, size=BLOCK):
    return pl.ds(pl.multiple_of(number * size, size), size)


def normalized(values):
    center = values - jnp.mean(values, axis=-1, keepdims=True)
    spread = jnp.mean(center * center, axis=-1, keepdims=True)
    scale = lax.rsqrt(spread + 1e-05)
    return center * scale, scale


GELU_A = 0.7978845608028654
GELU_B = 0.044715


def gelu_value(inner):
    return 0.5 * inner * (1.0 + jnp.tanh(GELU_A * (inner + GELU_B * inner * inner * inner)))


def gelu_both(inner):
    square = inner * inner
    bent = jnp.tanh(inner * (GELU_A + GELU_A * GELU_B * square))
    half = 0.5 + 0.5 * bent
    slope = half + 0.5 * inner * (1.0 - bent * bent) * (GELU_A + 3.0 * GELU_A * GELU_B * square)
    return inner * half, slope


def weight_copy(tiles, table, number, target, column, row, sem):
    depth, width = tiles.shape[1], tiles.shape[2]
    rows = pl.ds(pl.multiple_of(row * depth, depth), depth)
    columns = pl.ds(pl.multiple_of(column * width, width), width)
    return pltpu.make_async_copy(
        tiles.at[table[number]], target.at[rows, columns], sem.at[number]
    )


def weight_group(tiles, table, first, count, per_row, target, sem, act):
    @pl.loop(0, count)
    def _(j):
        copy = weight_copy(
            tiles, table, first + j, target, lax.rem(j, per_row), lax.div(j, per_row), sem
        )
        getattr(copy, act)()


def lane_is_first(shape):
    return lax.broadcasted_iota(jnp.int32, shape, 1) < shape[1] // 2


def stacked(values, lanes_first):
    zero = jnp.zeros_like(values)
    return jnp.concatenate(
        [
            jnp.where(lanes_first, values, zero).astype(BF16),
            jnp.where(lanes_first, zero, values).astype(BF16),
        ],
        axis=0,
    )


def forward_kernel(
    table, spans, norms, doc_row, hidden, tiles,
    below_out, normed_out, packed_out, mixed_out, logsum_out, middle_out, normed_two_out,
    hidden_out,
    w_qkv, w_out, w_up, w_down, flow, normed, packed, mixed, logcol, logsum, middle, normed_two,
    doc_col, w_sem, o_sem,
):
    length, width = hidden.shape
    blocks = length // DENSE
    pairs = mixed.shape[0]
    lanes = mixed.shape[2]
    groups = (
        (0, 12, 12, w_qkv), (12, 4, 4, w_out), (16, 16, 16, w_up), (32, 16, 4, w_down),
    )

    def fetch(layer, group, act):
        first, count, per_row, target = groups[group]
        weight_group(
            tiles, table, 48 * layer + first, count, per_row, target.at[layer], w_sem, act
        )

    for layer in range(LAYERS):
        for group in range(4):
            fetch(layer, group, "start")
    outs = (
        (normed, normed_out), (packed, packed_out), (mixed, mixed_out), (logsum, logsum_out),
        (middle, middle_out), (normed_two, normed_two_out), (flow, below_out),
    )

    def flush(number, layer):
        return pltpu.make_async_copy(outs[number][0], outs[number][1].at[layer], o_sem.at[number])

    def forward_one(layer):
        def again(number):
            pl.when(layer > 0)(lambda: flush(number, layer).wait())

        flush(6, layer).start()
        again(0)
        again(1)
        fetch(layer, 0, "wait")

        @pl.loop(0, blocks)
        def _(number):
            here = rows_of(number, DENSE)
            unit, _ = normalized(flow[here, :])
            low = (unit * norms[pl.ds(4 * layer + 0, 1), :] + norms[pl.ds(4 * layer + 1, 1), :]).astype(BF16)
            normed[here, :] = low
            product = dot_nn(low, w_qkv[layer])
            for j in range(3 * pairs):
                packed[j, here, :] = product[:, j * lanes : (j + 1) * lanes].astype(BF16)

        flush(0, layer).start()
        flush(1, layer).start()
        again(2)
        lane_ids = lax.broadcasted_iota(jnp.int32, (QUERY, lanes), 1)
        first_half = lane_is_first((QUERY, lanes))

        @pl.loop(0, length // QUERY)
        def _(number):
            here = rows_of(number, QUERY)
            low_key = spans[0, number]
            key_count = spans[1, number]
            doc_here = doc_col[here, 0:1]

            def with_keys(many):
                keys_here = pl.ds(pl.multiple_of(low_key * QUERY, QUERY), many * BLOCK)
                same = doc_here == doc_row[0:1, keys_here]
                same = jnp.concatenate([same, same], axis=0)

                def score(pair):
                    heads = stacked(packed[pair, here, :].astype(F32) * 0.125, first_half)
                    return dot_nt(heads, packed[pairs + pair, keys_here, :])

                def settle(scores):
                    scores = jnp.where(same, scores, -1e30)
                    top = jnp.max(scores, axis=-1, keepdims=True)
                    weights = jnp.exp(scores - top)
                    total = jnp.sum(weights, axis=-1, keepdims=True)
                    return weights.astype(BF16), total, top + jnp.log(total)

                def finish(pair, weights, total, logs):
                    result = dot_nn(weights, packed[2 * pairs + pair, keys_here, :]) / total
                    mixed[pair, here, :] = jnp.where(
                        first_half, result[:QUERY], result[QUERY:]
                    ).astype(BF16)
                    old = logcol[here, :]
                    old = jnp.where(lane_ids == 8 * pair, logs[:QUERY], old)
                    logcol[here, :] = jnp.where(lane_ids == 8 * pair + 1, logs[QUERY:], old)

                waiting = None
                ahead = score(0)
                for pair in range(pairs):
                    now = ahead
                    if pair + 1 < pairs:
                        ahead = score(pair + 1)
                    done = settle(now)
                    if waiting is not None:
                        finish(pair - 1, *waiting)
                    waiting = done
                finish(pairs - 1, *waiting)


            for many in range(1, length // BLOCK + 1):
                pl.when(key_count == many)(lambda many=many: with_keys(many))

        flush(2, layer).start()
        turned = logcol[...].T
        again(3)
        for pair in range(pairs):
            logsum[pair, :, :] = turned[8 * pair : 8 * pair + 8, :]
        flush(3, layer).start()
        fetch(layer, 1, "wait")
        fetch(layer, 2, "wait")
        fetch(layer, 3, "wait")
        again(4)
        again(5)
        flush(6, layer).wait()
        chunk = width

        @pl.loop(0, blocks)
        def _(number):
            here = rows_of(number, DENSE)
            side_by_side = jnp.concatenate([mixed[pair, here, :] for pair in range(pairs)], axis=1)
            mid = flow[here, :] + dot_nn(side_by_side, w_out[layer])
            middle[here, :] = mid
            unit, _ = normalized(mid)
            low = (unit * norms[pl.ds(4 * layer + 2, 1), :] + norms[pl.ds(4 * layer + 3, 1), :]).astype(BF16)
            normed_two[here, :] = low
            total = mid
            for c in range(w_up.shape[2] // chunk):
                part = slice(c * chunk, (c + 1) * chunk)
                active = gelu_value(dot_nn(low, w_up[layer, :, part])).astype(BF16)
                total = total + dot_nn(active, w_down[layer, part, :])
            flow[here, :] = total

        flush(4, layer).start()
        flush(5, layer).start()

    flow[...] = hidden[...].astype(F32)
    fill_columns(doc_row, doc_col)

    @pl.loop(0, LAYERS)
    def _(layer):
        forward_one(layer)

    last = pltpu.make_async_copy(normed, hidden_out, o_sem.at[7])
    flush(0, LAYERS - 1).wait()
    normed[...] = flow[...].astype(BF16)
    last.start()
    for number in range(1, 6):
        flush(number, LAYERS - 1).wait()
    last.wait()


def fill_columns(doc_row, doc_col):
    lanes = doc_col.shape[1]

    @pl.loop(0, doc_col.shape[0] // lanes)
    def _(number):
        here = rows_of(number, lanes)
        spread = jnp.broadcast_to(doc_row[0:1, here].astype(F32), (lanes, lanes))
        doc_col[here, :] = spread.T.astype(jnp.int32)


def vmem_spec():
    return pl.BlockSpec(memory_space=pltpu.VMEM)


def any_spec():
    return pl.BlockSpec(memory_space=pl.ANY)


def smem_spec():
    return pl.BlockSpec(memory_space=pltpu.SMEM)


def forward_layers(table, spans, norms, doc_row, hidden, tiles, pairs):
    length, width = hidden.shape
    lanes = tiles.shape[2]
    one = (
        ((length, width), F32),
        ((length, width), BF16),
        ((3 * pairs, length, lanes), BF16),
        ((pairs, length, lanes), BF16),
        ((pairs, 8, length), F32),
        ((length, width), F32),
        ((length, width), BF16),
    )
    shapes = [((LAYERS, *s), d) for s, d in one] + [((length, width), BF16)]
    keep = [pltpu.VMEM(s, d) for s, d in one]
    return pl.pallas_call(
        forward_kernel,
        name="forward_layers",
        out_shape=[jax.ShapeDtypeStruct(s, d) for s, d in shapes],
        in_specs=[smem_spec(), smem_spec()] + [vmem_spec()] * 3 + [any_spec()],
        out_specs=[any_spec()] * len(shapes),
        scratch_shapes=[
            pltpu.VMEM((LAYERS, width, 3 * width), BF16),
            pltpu.VMEM((LAYERS, width, width), BF16),
            pltpu.VMEM((LAYERS, width, 4 * width), BF16),
            pltpu.VMEM((LAYERS, 4 * width, width), BF16),
            *keep[:4],
            pltpu.VMEM((length, lanes), F32),
            *keep[4:],
            pltpu.VMEM((length, lanes), jnp.int32),
            pltpu.SemaphoreType.DMA((48 * LAYERS,)),
            pltpu.SemaphoreType.DMA((8,)),
        ],
        compiler_params=pltpu.CompilerParams(vmem_limit_bytes=VMEM_BYTES),
        cost_estimate=pl.CostEstimate(
            flops=length * width * width * 52, bytes_accessed=40 * 2**20,
            transcendentals=length * length * 8,
        ),
    )(table, spans, norms, doc_row, hidden, tiles)


def backward_kernel(
    table, aims, spans, counts, norms, doc_row, upper_in,
    below_in, normed_in, packed_in, mixed_in, logsum_in, middle_in, normed_two_in, tiles,
    grad_out, tile_grads, norm_grads,
    w_qkv, w_out, w_up, w_down,
    flow, normed, packed, mixed, logsum, middle, normed_two, hidden,
    active, inner_grad, grad_low, mid_grad, mid_low, mixed_grad, delta, packed_grad,
    key_sum, value_sum, staged, blank, doc_col, selector,
    w_sem, i_sem, t_sem, z_sem, o_sem,
):
    length, width = flow.shape
    blocks = length // DENSE_BACK
    pairs, lanes = mixed.shape[0], mixed.shape[2]
    groups = (
        (0, 12, 12, w_qkv), (12, 4, 4, w_out), (16, 16, 16, w_up), (32, 16, 4, w_down),
    )
    ins = (
        (normed_two_in, normed_two), (middle_in, middle), (mixed_in, mixed),
        (packed_in, packed), (logsum_in, logsum), (below_in, hidden), (normed_in, normed),
    )

    def load(number, layer):
        return pltpu.make_async_copy(ins[number][0].at[layer], ins[number][1], i_sem.at[number])

    def fetch(group, layer, act):
        first, count, per_row, target = groups[group]
        weight_group(tiles, table, 48 * layer + first, count, per_row, target, w_sem, act)

    def early(layer):
        load(0, layer).start()
        fetch(2, layer, "start")
        fetch(3, layer, "start")
        load(1, layer).start()
        fetch(1, layer, "start")
        load(2, layer).start()

    def late(layer):
        load(3, layer).start()
        load(4, layer).start()

    take = pltpu.make_async_copy(upper_in, grad_low, o_sem.at[0])
    take.start()
    early(LAYERS - 1)
    late(LAYERS - 1)
    fetch(0, LAYERS - 1, "start")
    load(5, LAYERS - 1).start()
    load(6, LAYERS - 1).start()

    def blank_copies(act):
        capacity = tile_grads.shape[0] // counts.shape[0]
        quarter = capacity // 4

        @pl.loop(0, counts.shape[0])
        def _(owner):
            @pl.loop(counts[owner], capacity)
            def _(place):
                core, depth_z, part = lax.rem(owner, 2), lax.div(owner, 2), lax.div(place, quarter)
                low_bit, high_bit = lax.rem(part, 2), lax.div(part, 2)
                major = low_bit + core * (high_bit - low_bit)
                minor = high_bit + core * (low_bit - high_bit)
                index = lax.rem(place, quarter) * 32 + core * 16 + major * 8 + minor * 4 + depth_z
                getattr(
                    pltpu.make_async_copy(blank, tile_grads.at[index], z_sem.at[index]), act
                )()

    norm_grads[...] = jnp.zeros_like(norm_grads)
    blank[...] = jnp.zeros_like(blank)
    fill_columns(doc_row, doc_col)
    which = lax.broadcasted_iota(jnp.int32, selector.shape, 0)
    lane = lax.broadcasted_iota(jnp.int32, selector.shape, 1)
    head_dim = width // HEADS
    own_head = 2 * lax.div(which, 8) + lax.rem(which, 8)
    fits = (lax.rem(which, 8) < 2) & (lax.div(lane, head_dim) == own_head)
    selector[...] = jnp.where(fits, 1.0, 0.0)
    take.wait()
    flow[...] = grad_low[...].astype(F32)
    chunk = 2 * width
    chunks = w_up.shape[1] // chunk

    def send_tile(place, layer):
        return pltpu.make_async_copy(
            staged.at[place], tile_grads.at[aims[48 * layer + place]], t_sem.at[place]
        )

    def settle_tiles(layer):
        @pl.loop(0, 48)
        def _(place):
            send_tile(place, layer).wait()

    def backward_one(layer):
        def norm_back(values, out_grad, gain, gain_row):
            unit, scale = normalized(values)
            sums = (
                jnp.sum(out_grad * unit, axis=0, keepdims=True),
                jnp.sum(out_grad, axis=0, keepdims=True),
            )
            for which in range(LAYERS):

                @pl.when(layer == which)
                def _(which=which):
                    for side in range(2):
                        row = 4 * which + gain_row + side
                        norm_grads[row : row + 1, :] += sums[side]

            turned = out_grad * gain
            average = jnp.mean(turned, axis=-1, keepdims=True)
            along = jnp.mean(turned * unit, axis=-1, keepdims=True)
            return scale * (turned - average - unit * along)

        load(0, layer).wait()
        fetch(2, layer, "wait")
        fetch(3, layer, "wait")
        load(1, layer).wait()
        fetch(1, layer, "wait")
        load(2, layer).wait()

        @pl.loop(0, blocks)
        def _(number):
            here = rows_of(number, DENSE_BACK)
            upper = flow[here, :]
            low = upper.astype(BF16)
            grad_low[here, :] = low
            normed_here = normed_two[here, :]
            total = jnp.zeros((DENSE_BACK, width), F32)
            for c in range(chunks):
                part = slice(c * chunk, (c + 1) * chunk)
                value, slope = gelu_both(dot_nn(normed_here, w_up[:, part]))
                active[here, part] = value.astype(BF16)
                inner = (slope * dot_nt(low, w_down[part, :])).astype(BF16)
                inner_grad[here, part] = inner
                total = total + dot_nt(inner, w_up[:, part])
            mid = upper + norm_back(middle[here, :], total, norms[pl.ds(4 * layer + 2, 1), :], 2)
            mid_grad[here, :] = mid
            mid_here = mid.astype(BF16)
            mid_low[here, :] = mid_here
            back = dot_nt(mid_here, w_out[...]).astype(BF16)
            for pair in range(pairs):
                mixed_grad[pair, here, :] = back[:, pair * lanes : (pair + 1) * lanes]
            side_by_side = jnp.concatenate([mixed[pair, here, :] for pair in range(pairs)], axis=1)
            both = side_by_side.astype(F32) * back.astype(F32)
            sums = dot_nt(selector[...], both, precision=lax.Precision.HIGHEST)
            for pair in range(pairs):
                delta[pair, :, here] = sums[8 * pair : 8 * pair + 8, :]

        pl.when(layer < LAYERS - 1)(lambda: settle_tiles(layer + 1))

        def emit(block, first):
            for c in range(block.shape[1] // lanes):
                staged[first + c] = block[:, c * lanes : (c + 1) * lanes].astype(BF16)
                send_tile(first + c, layer).start()

        @pl.loop(0, 4)
        def _(c):
            part = rows_of(c, width)
            emit(dot_tn(active[:, part], grad_low[...]), 32 + 4 * c)
            emit(dot_tn(normed_two[...], inner_grad[:, part]), 16 + 4 * c)

        side_by_side = jnp.concatenate([mixed[pair] for pair in range(pairs)], axis=1)
        emit(dot_tn(side_by_side, mid_low[...]), 12)
        pl.when(layer > 0)(lambda: early(layer - 1))
        pl.when(layer == LAYERS - 1)(lambda: blank_copies("start"))
        load(3, layer).wait()
        load(4, layer).wait()
        first_half = lane_is_first((QUERY, lanes))

        key_sum[...] = jnp.zeros_like(key_sum)
        value_sum[...] = jnp.zeros_like(value_sum)

        @pl.loop(0, length // QUERY)
        def _(number):
            here = rows_of(number, QUERY)
            low_key = spans[0, number]
            key_count = spans[1, number]
            doc_here = doc_row[0:1, here]
            doc_here = jnp.concatenate([doc_here, doc_here], axis=1)

            def with_keys(many):
                keys_here = pl.ds(pl.multiple_of(low_key * QUERY, QUERY), many * BLOCK)
                same = doc_col[keys_here, 0:1] == doc_here

                def score(pair):
                    heads = stacked(packed[pair, here, :].astype(F32) * 0.125, first_half)
                    outs = stacked(mixed_grad[pair, here, :].astype(F32), first_half)
                    return (
                        heads,
                        outs,
                        dot_nt(packed[pairs + pair, keys_here, :], heads),
                        dot_nt(packed[2 * pairs + pair, keys_here, :], outs),
                    )

                def settle(pair, heads, outs, scores, from_values):
                    logs = jnp.concatenate([logsum[pair, 0:1, here], logsum[pair, 1:2, here]], axis=1)
                    means = jnp.concatenate([delta[pair, 0:1, here], delta[pair, 1:2, here]], axis=1)
                    weights = jnp.exp(jnp.where(same, scores - logs, -1e30))
                    score_grad = (weights * (from_values - means)).astype(BF16)
                    return heads, outs, weights.astype(BF16), score_grad

                def finish(pair, heads, outs, weights, score_grad):
                    value_sum[pair, keys_here, :] += dot_nn(weights, outs)
                    key_sum[pair, keys_here, :] += dot_nn(score_grad, heads)
                    query_part = dot_tn(score_grad, packed[pairs + pair, keys_here, :]) * 0.125
                    packed_grad[pair, here, :] = jnp.where(
                        first_half, query_part[:QUERY], query_part[QUERY:]
                    ).astype(BF16)

                waiting = None
                ahead = score(0)
                for pair in range(pairs):
                    now = ahead
                    if pair + 1 < pairs:
                        ahead = score(pair + 1)
                    done = settle(pair, *now)
                    if waiting is not None:
                        finish(pair - 1, *waiting)
                    waiting = done
                finish(pairs - 1, *waiting)

            for many in range(1, length // BLOCK + 1):
                pl.when(key_count == many)(lambda many=many: with_keys(many))

        for pair in range(pairs):
            packed_grad[pairs + pair] = key_sum[pair].astype(BF16)
            packed_grad[2 * pairs + pair] = value_sum[pair].astype(BF16)

        pl.when(layer > 0)(lambda: late(layer - 1))
        fetch(0, layer, "wait")
        load(5, layer).wait()
        load(6, layer).wait()

        @pl.loop(0, blocks)
        def _(number):
            here = rows_of(number, DENSE_BACK)
            wide = jnp.concatenate([packed_grad[j, here, :] for j in range(3 * pairs)], axis=1)
            total = dot_nt(wide, w_qkv[...])
            flow[here, :] = mid_grad[here, :] + norm_back(
                hidden[here, :], total, norms[pl.ds(4 * layer + 0, 1), :], 0
            )

        @pl.loop(0, 3)
        def _(c):
            wide = jnp.concatenate([packed_grad[pairs * c + j] for j in range(pairs)], axis=1)
            emit(dot_tn(normed[...], wide), 4 * c)

        @pl.when(layer > 0)
        def _():
            fetch(0, layer - 1, "start")
            load(5, layer - 1).start()
            load(6, layer - 1).start()

    @pl.loop(0, LAYERS)
    def _(step):
        backward_one(LAYERS - 1 - step)

    flush = pltpu.make_async_copy(grad_low, grad_out, o_sem.at[0])
    grad_low[...] = flow[...].astype(BF16)
    flush.start()
    settle_tiles(0)
    flush.wait()
    blank_copies("wait")


def backward_layers(
    table, aims, spans, counts, norms, doc_row, upper, saved, tiles
):
    length, width = upper.shape
    lanes = tiles.shape[2]
    pairs = width // lanes
    slots = tiles.shape[0]
    return pl.pallas_call(
        backward_kernel,
        name="backward_layers",
        out_shape=[
            jax.ShapeDtypeStruct((length, width), BF16),
            jax.ShapeDtypeStruct(tiles.shape, BF16),
            jax.ShapeDtypeStruct(norms.shape, F32),
        ],
        in_specs=[smem_spec()] * 4 + [vmem_spec()] * 2 + [any_spec()] * 9,
        out_specs=[any_spec(), any_spec(), vmem_spec()],
        scratch_shapes=[
            pltpu.VMEM((width, 3 * width), BF16),
            pltpu.VMEM((width, width), BF16),
            pltpu.VMEM((width, 4 * width), BF16),
            pltpu.VMEM((4 * width, width), BF16),
            pltpu.VMEM((length, width), F32),
            pltpu.VMEM((length, width), BF16),
            pltpu.VMEM((3 * pairs, length, lanes), BF16),
            pltpu.VMEM((pairs, length, lanes), BF16),
            pltpu.VMEM((pairs, 8, length), F32),
            pltpu.VMEM((length, width), F32),
            pltpu.VMEM((length, width), BF16),
            pltpu.VMEM((length, width), F32),
            pltpu.VMEM((length, 4 * width), BF16),
            pltpu.VMEM((length, 4 * width), BF16),
            pltpu.VMEM((length, width), BF16),
            pltpu.VMEM((length, width), F32),
            pltpu.VMEM((length, width), BF16),
            pltpu.VMEM((pairs, length, lanes), BF16),
            pltpu.VMEM((pairs, 8, length), F32),
            pltpu.VMEM((3 * pairs, length, lanes), BF16),
            pltpu.VMEM((pairs, length, lanes), F32),
            pltpu.VMEM((pairs, length, lanes), F32),
            pltpu.VMEM((48, width, lanes), BF16),
            pltpu.VMEM((width, lanes), BF16),
            pltpu.VMEM((length, lanes), jnp.int32),
            pltpu.VMEM((8 * pairs, width), F32),
            pltpu.SemaphoreType.DMA((48 * LAYERS,)),
            pltpu.SemaphoreType.DMA((7,)),
            pltpu.SemaphoreType.DMA((48,)),
            pltpu.SemaphoreType.DMA((slots,)),
            pltpu.SemaphoreType.DMA((1,)),
        ],
        compiler_params=pltpu.CompilerParams(vmem_limit_bytes=VMEM_BYTES),
        cost_estimate=pl.CostEstimate(
            flops=length * width * width * 120, bytes_accessed=60 * 2**20,
            transcendentals=length * length * 8,
        ),
    )(
        table, aims, spans, counts, norms, doc_row, upper, *saved, tiles
    )


MESH_IDS = pl.DeviceIdType.MESH


def place_of_device():
    row = lax.axis_index("rows")
    seat = lax.axis_index("seq")
    return row % 2, row // 2, seat // 2, seat % 2


def device_at(x, y, z, core):
    return (2 * y + x, 2 * z + core)


def greet(partners):
    barrier = pltpu.get_barrier_semaphore()
    for partner in partners:
        pl.semaphore_signal(barrier, inc=1, device_id=partner, device_id_type=MESH_IDS)
    pl.semaphore_wait(barrier, len(partners))


def seat_partners(x, y, z, core):
    others = []
    for k in range(1, 8):
        seat = (2 * z + core + k) % 8
        others.append((2 * y + x, seat))
    return others


def post(source, target, send_sem, recv_sem, number, partner):
    copy = pltpu.make_async_remote_copy(
        src_ref=source,
        dst_ref=target,
        send_sem=send_sem.at[number],
        recv_sem=recv_sem.at[number],
        device_id=partner,
        device_id_type=MESH_IDS,
    )
    copy.start()
    return copy


def gather_kernel(master, residual, tiles, rows, wide, low, flat, flat_low, send_sem, recv_sem, l_sem):
    x, y, z, core = place_of_device()
    quarter_id = 2 * y + x
    across = device_at(x, y, z, 1 - core)
    by_x = device_at(1 - x, y, z, core)
    by_y = device_at(x, 1 - y, z, core)
    quarters = (quarter_id, 2 * y + (1 - x), 2 * (1 - y) + x, 3 - quarter_id)
    seats = seat_partners(x, y, z, core)
    seat = 2 * z + core
    load_near = pltpu.make_async_copy(
        master.at[pl.ds(4 * quarter_id, 4)], wide.at[pl.ds(4 * quarter_id, 4)], l_sem.at[0]
    )
    load_near.start()
    far = []
    for k in range(1, 4):
        part = pl.ds(4 * ((quarter_id + k) % 4), 4)
        copy = pltpu.make_async_copy(master.at[part], wide.at[part], l_sem.at[1 + k])
        copy.start()
        far.append(copy)
    load_flat = pltpu.make_async_copy(residual, flat, l_sem.at[1])
    load_flat.start()
    greet(seats + [by_x, by_y])

    def spot(z_from, quarter):
        return core * 64 + z_from * 16 + 4 * quarter

    def convert(first, count):
        @pl.loop(0, count)
        def _(j):
            low[first + j] = wide[first + j].astype(BF16)

    def make(source, target, number, partner):
        return pltpu.make_async_remote_copy(
            src_ref=source, dst_ref=target, send_sem=send_sem.at[number],
            recv_sem=recv_sem.at[number], device_id=partner, device_id_type=MESH_IDS,
        )

    def relay(number, first, count, partner):
        part = pl.ds(first, count)
        return make(tiles.at[part], tiles.at[part], number, partner)

    mine = pl.ds(core * 64 + z * 16, 16)
    own_here = pl.ds(spot(z, quarter_id), 4)

    def hop(way, step):
        toward = device_at(x, y, lax.rem(z + (1 if way == 0 else 3), 4), core)
        number = 3 * way + step - 1
        if step == 1:
            return make(low.at[pl.ds(4 * quarter_id, 4)], tiles.at[own_here], number, toward)
        z_from = lax.rem(z + (5 - step if way == 0 else step - 1), 4)
        return relay(number, spot(z_from, quarter_id), 4, toward)

    def can_send(way, step):
        if way == 0:
            return (z < 3) & (z >= step - 1)
        return (z > 0) & (z <= 4 - step)

    def arrives(way, step):
        return z >= step if way == 0 else z <= 3 - step

    def source(way, step):
        return lax.rem(z + (4 - step if way == 0 else step), 4)

    steps = [(way, step) for step in range(1, 4) for way in range(2)]

    def fan(way, step):
        base = 6 + 9 * (3 * way + step - 1)
        z_from = source(way, step)
        return [
            relay(base, spot(z_from, quarters[0]), 4, by_x),
            relay(base + 1, spot(z_from, quarters[0]), 4, by_y),
            relay(base + 2, spot(z_from, quarters[0]), 4, across),
            relay(base + 3, spot(z_from, quarters[1]), 2, by_y),
            relay(base + 4, spot(z_from, quarters[1]), 4, across),
            relay(base + 5, spot(z_from, quarters[2]) + 2, 2, by_x),
            relay(base + 6, spot(z_from, quarters[2]), 4, across),
            relay(base + 7, spot(z_from, quarters[3]), 2, across),
            relay(base + 8, spot(z_from, quarters[3]) + 2, 2, across),
        ]

    load_near.wait()
    convert(4 * quarter_id, 4)
    for way in range(2):
        pl.when(can_send(way, 1))(lambda way=way: hop(way, 1).start())
    for k in range(1, 4):
        far[k - 1].wait()
        convert(4 * ((quarter_id + k) % 4), 4)
    keep_tiles = pltpu.make_async_copy(low, tiles.at[mine], l_sem.at[6])
    keep_tiles.start()
    own_across = make(low, tiles.at[mine], 60, across)
    own_across.start()
    load_flat.wait()

    @pl.loop(0, flat.shape[0])
    def _(j):
        flat_low[j] = flat[j].astype(BF16)

    keep_row = pltpu.make_async_copy(flat_low.at[seat], rows.at[seat], l_sem.at[5])
    keep_row.start()
    row_moves = [
        make(flat_low.at[(seat + k) % 8], rows.at[seat], 60 + k, seats[k - 1])
        for k in range(1, 8)
    ]

    def take(way, step):
        hop(way, step).wait_recv()
        if step < 3:
            pl.when(can_send(way, step + 1))(lambda: hop(way, step + 1).start())
        for copy in fan(way, step)[:3]:
            copy.start()

    def turn(way, step):
        moves = fan(way, step)
        moves[0].wait_recv()
        moves[3].start()
        moves[4].start()
        moves[1].wait_recv()
        moves[5].start()
        moves[6].start()

    def finish(way, step):
        moves = fan(way, step)
        moves[3].wait_recv()
        moves[7].start()
        moves[5].wait_recv()
        moves[8].start()

    def drain(way, step):
        moves = fan(way, step)
        for number in (2, 4, 6, 7, 8):
            moves[number].wait_recv()
        for copy in moves:
            copy.wait_send()

    def each(act, chosen):
        for way, step in chosen:
            pl.when(arrives(way, step))(lambda way=way, step=step: act(way, step))

    each(take, steps[:2])
    each(take, steps[2:4])
    each(turn, steps[:2])
    each(take, steps[4:])
    for copy in row_moves:
        copy.start()
    each(turn, steps[2:4])
    each(finish, steps[:2])
    each(turn, steps[4:])
    each(finish, steps[2:])
    own_across.wait_recv()
    each(drain, steps)
    for way, step in steps:
        pl.when(can_send(way, step))(lambda way=way, step=step: hop(way, step).wait_send())
    for copy in row_moves:
        copy.wait_recv()
        copy.wait_send()
    own_across.wait_send()
    keep_row.wait()
    keep_tiles.wait()


def gather_start(master_tiles, residual):
    capacity, depth, lanes = master_tiles.shape
    count = 68
    return pl.pallas_call(
        gather_kernel,
        name="gather_start",
        out_shape=[
            jax.ShapeDtypeStruct((8 * capacity, depth, lanes), BF16),
            jax.ShapeDtypeStruct(residual.shape, BF16),
        ],
        in_specs=[any_spec()] * 2,
        out_specs=[any_spec()] * 2,
        scratch_shapes=[
            pltpu.VMEM(master_tiles.shape, F32),
            pltpu.VMEM(master_tiles.shape, BF16),
            pltpu.VMEM(residual.shape, F32),
            pltpu.VMEM(residual.shape, BF16),
            pltpu.SemaphoreType.DMA((count,)),
            pltpu.SemaphoreType.DMA((count,)),
            pltpu.SemaphoreType.DMA((7,)),
        ],
        compiler_params=pltpu.CompilerParams(
            collective_id=0, has_side_effects=True, vmem_limit_bytes=VMEM_BYTES
        ),
        cost_estimate=pl.CostEstimate(
            flops=0, bytes_accessed=200 * 2**20, transcendentals=0
        ),
    )(master_tiles, residual)


def reduce_kernel(
    held, upper, norm_part, owned, rows, norm_sum, squares,
    core_in, own, one_in, two_in, z_in, piece, norm_in, norm_now, square_in,
    square_now, send_sem, recv_sem, l_sem,
):
    x, y, z, core = place_of_device()
    quarter_id = 2 * y + x
    across = device_at(x, y, z, 1 - core)
    by_x = device_at(1 - x, y, z, core)
    by_y = device_at(x, 1 - y, z, core)
    by_both = device_at(1 - x, 1 - y, z, core)
    plus, minus = core, 1 - core
    first_bit = x * minus + y * plus
    second_bit = y * minus + x * plus
    one = device_at(x + minus * (1 - 2 * x), y + plus * (1 - 2 * y), z, core)
    two = device_at(x + plus * (1 - 2 * x), y + minus * (1 - 2 * y), z, core)
    along_z = [device_at(x, y, (z + k) % 4, core) for k in range(1, 4)]
    seats = seat_partners(x, y, z, core)
    seat = 2 * z + core
    quarter_x, quarter_y = 2 * y + (1 - x), 2 * (1 - y) + x
    chunks = own.shape[0]
    number = 0
    copies = []

    def move(source, target, partner):
        nonlocal number
        copy = post(source, target, send_sem, recv_sem, number, partner)
        number += 1
        copies.append(copy)
        return copy

    loads = []
    for i in range(chunks):
        copy = pltpu.make_async_copy(
            held.at[pl.ds(32 * i + 16 * core, 16)], own.at[i], l_sem.at[i]
        )
        copy.start()
        loads.append(copy)
    greet(seats + [by_x, by_y, by_both])
    half = own.shape[2] // 2
    parts = [(i, pl.ds(half * side, half)) for i in range(chunks) for side in range(2)]
    core_moves = [
        move(held.at[pl.ds(32 * i + 16 * (1 - core), 16), rows_], core_in.at[i, :, rows_], across)
        for i, rows_ in parts
    ]
    norm_now[0] = norm_part[...]
    norm_moves = [move(norm_now.at[0], norm_in.at[0], across)]
    for k in range(1, 8):
        move(upper.at[(seat + k) % 8], rows.at[seat], seats[k - 1])
    row_moves = copies[-7:]
    keep_row = pltpu.make_async_copy(upper.at[seat], rows.at[seat], l_sem.at[chunks])
    keep_row.start()

    def add_in(target, first, incoming, count, part):
        @pl.loop(0, count)
        def _(j):
            target[first + j, part, :] = (
                target[first + j, part, :].astype(F32) + incoming[j, part, :].astype(F32)
            ).astype(BF16)

    one_moves, two_moves, z_moves, near_moves, corner_moves, keeps = [], [], [], [], [], []

    def stage_core(n):
        i, part = parts[n]
        if n % 2 == 0:
            loads[i].wait()
        core_moves[n].wait_recv()
        add_in(own.at[i], 0, core_in.at[i], 16, part)
        one_moves.append(
            move(
                own.at[i, pl.ds(8 * (1 - first_bit), 8), part], one_in.at[i, :, part], one
            )
        )

    def stage_one(n):
        i, part = parts[n]
        one_moves[n].wait_recv()
        add_in(own.at[i], 8 * first_bit, one_in.at[i], 8, part)
        two_moves.append(
            move(
                own.at[i, pl.ds(8 * first_bit + 4 * (1 - second_bit), 4), part],
                two_in.at[i, :, part],
                two,
            )
        )

    def stage_two(n):
        i, part = parts[n]
        two_moves[n].wait_recv()
        base = 8 * first_bit + 4 * second_bit
        add_in(own.at[i], base, two_in.at[i], 4, part)
        z_moves.append(
            [
                move(
                    own.at[i, base + (z + k) % 4, part], z_in.at[i, k - 1, part], along_z[k - 1]
                )
                for k in range(1, 4)
            ]
        )

    def stage_z(n):
        i, part = parts[n]
        for copy in z_moves[n]:
            copy.wait_recv()
        total = own[i, 8 * first_bit + 4 * second_bit + z, part, :].astype(F32)
        for k in range(3):
            total = total + z_in[i, k, part, :].astype(F32)
        piece[i, part, :] = total.astype(BF16)
        square_now[0] += jnp.sum((total * total).reshape(-1, 8, total.shape[1]), axis=0)
        here = owned.at[4 * quarter_id + i, part]
        near_moves.append(
            [move(piece.at[i, part], here, partner) for partner in (by_x, by_y)]
        )
        if n >= len(parts) - 2:
            corner_moves.append(move(piece.at[i, part], here, by_both))
        keep = pltpu.make_async_copy(piece.at[i, part], here, l_sem.at[chunks + 1 + n])
        keep.start()
        keeps.append(keep)

    def stage_turn(n):
        i, part = parts[n]
        side = n % 2
        near_moves[n][1 - side].wait_recv()
        far_id = quarter_y if side == 0 else quarter_x
        here = owned.at[4 * far_id + i, part]
        corner_moves.append(move(here, here, by_x if side == 0 else by_y))

    def norm_stage(step, partner):
        norm_moves[step].wait_recv()
        norm_now[step + 1] = norm_now[step] + norm_in[step]
        if partner is not None:
            norm_moves.append(move(norm_now.at[step + 1], norm_in.at[step + 1], partner))

    square_now[...] = jnp.zeros_like(square_now)
    for n in range(8):
        stage_core(n)
        if n == 1:
            norm_stage(0, by_x)
        if n == 3:
            norm_stage(1, by_y)
        if n == 5:
            norm_stage(2, None)
    norm_z = [move(norm_now.at[3], norm_in.at[2 + k], along_z[k - 1]) for k in range(1, 4)]
    for n in range(8 + 5):
        if n < 8:
            stage_one(n)
        if 0 <= n - 1 < 8:
            stage_two(n - 1)
        if 0 <= n - 3 < 8:
            stage_z(n - 3)
        if 0 <= n - 5 < 6:
            stage_turn(n - 5)

    def in_order(own_value, incoming):
        values = [own_value] + [incoming(k) for k in range(1, 4)]
        total = None
        for place in range(4):
            picked = values[0]
            for k in range(1, 4):
                picked = jnp.where((z + 4 - k) % 4 == place, values[k], picked)
            total = picked if total is None else total + picked
        return total

    square_moves = []

    def square_stage(step, partner):
        square_moves.append(move(square_now.at[step], square_in.at[step], partner))
        square_moves[step].wait_recv()
        square_now[step + 1] = square_now[step] + square_in[step]

    square_stage(0, by_x)
    square_stage(1, by_y)
    square_stage(2, across)
    square_z = [
        move(square_now.at[3], square_in.at[2 + k], along_z[k - 1]) for k in range(1, 4)
    ]
    for copy in norm_z:
        copy.wait_recv()
    norm_sum[...] = in_order(norm_now[3], lambda k: norm_in[2 + k])
    for copy in square_z:
        copy.wait_recv()
    squares[...] = in_order(square_now[3], lambda k: square_in[2 + k])
    straight = [near_moves[n][n % 2] for n in range(6)] + near_moves[6] + near_moves[7]
    for copy in row_moves + straight + corner_moves:
        copy.wait_recv()
    for copy in copies:
        copy.wait_send()
    keep_row.wait()
    for keep in keeps:
        keep.wait()


def reduce_end(held, upper, norm_part):
    slots, depth, lanes = held.shape
    chunks = 4
    count = 8 + 1 + 7 + 8 + 8 + 24 + 24 + 2 + 3 + 3 + 3
    return pl.pallas_call(
        reduce_kernel,
        name="reduce_end",
        out_shape=[
            jax.ShapeDtypeStruct((slots // 8, depth, lanes), BF16),
            jax.ShapeDtypeStruct(upper.shape, BF16),
            jax.ShapeDtypeStruct(norm_part.shape, F32),
            jax.ShapeDtypeStruct((8, lanes), F32),
        ],
        in_specs=[any_spec(), any_spec(), vmem_spec()],
        out_specs=[any_spec(), any_spec(), vmem_spec(), vmem_spec()],
        scratch_shapes=[
            pltpu.VMEM((chunks, 16, depth, lanes), BF16),
            pltpu.VMEM((chunks, 16, depth, lanes), BF16),
            pltpu.VMEM((chunks, 8, depth, lanes), BF16),
            pltpu.VMEM((chunks, 4, depth, lanes), BF16),
            pltpu.VMEM((chunks, 3, depth, lanes), BF16),
            pltpu.VMEM((chunks, depth, lanes), BF16),
            pltpu.VMEM((6, *norm_part.shape), F32),
            pltpu.VMEM((4, *norm_part.shape), F32),
            pltpu.VMEM((6, 8, lanes), F32),
            pltpu.VMEM((4, 8, lanes), F32),
            pltpu.SemaphoreType.DMA((count,)),
            pltpu.SemaphoreType.DMA((count,)),
            pltpu.SemaphoreType.DMA((3 * chunks + 1,)),
        ],
        compiler_params=pltpu.CompilerParams(
            collective_id=1, has_side_effects=True, vmem_limit_bytes=40 * 2**20
        ),
        cost_estimate=pl.CostEstimate(
            flops=0, bytes_accessed=300 * 2**20, transcendentals=0
        ),
    )(held, upper, norm_part)


def finish_kernel(
    counts, owned, master, first, second, grad_rows, out_rows, squares, norm_sum, norm_params,
    norm_first, norm_second,
    clip_out, first_out, second_out, master_out, copy_out, grad_rows_out, out_rows_out,
    total_out, norm_clip_out, norm_first_out, norm_second_out, norm_params_out,
    clip, new_first, new_second, new_master, new_copy, wide_grad, wide_out, o_sem,
):
    norms = norm_sum[...]
    total = jnp.sqrt(jnp.sum(squares[...]) + jnp.sum(norms * norms))
    factor = 1.0 / jnp.maximum(total, 1.0)
    correction = 1.0 - 0.5**STEP

    def step(weight, grad, low, high, rate):
        low = 0.5 * low + 0.5 * grad
        high = 0.5 * high + 0.5 * grad * grad
        update = low / correction / (jnp.sqrt(high / correction) + 1e-08)
        return weight - rate * (update + 0.01 * weight), low, high

    outs = (
        (clip, clip_out), (new_first, first_out), (new_second, second_out),
        (new_master, master_out), (new_copy, copy_out),
    )
    capacity = master.shape[0]

    def send(number, place):
        return pltpu.make_async_copy(
            outs[number][0].at[place], outs[number][1].at[place],
            o_sem.at[number * capacity + place],
        )

    count = counts[lax.axis_index("seq")]

    @pl.loop(0, capacity)
    def _(place):
        keep = (lax.broadcast(place, clip.shape[1:])) < count
        grad = jnp.where(keep, owned[place].astype(F32), 0.0) * factor
        weight, low, high = step(master[place], grad, first[place], second[place], 0.05)
        weight = jnp.where(keep, weight, 0.0)
        clip[place] = grad
        new_first[place] = jnp.where(keep, low, 0.0)
        new_second[place] = jnp.where(keep, high, 0.0)
        new_master[place] = weight
        new_copy[place] = weight.astype(BF16)
        for number in range(len(outs)):
            send(number, place).start()

    moves = []
    for number, (low, wide, target) in enumerate(
        ((grad_rows, wide_grad, grad_rows_out), (out_rows, wide_out, out_rows_out))
    ):

        @pl.loop(0, low.shape[0])
        def _(j, low=low, wide=wide):
            wide[j] = low[j].astype(F32)

        moves.append(pltpu.make_async_copy(wide, target, o_sem.at[5 * capacity + number]))
        moves[-1].start()
    clipped = norms * factor
    weight, low, high = step(norm_params[...], clipped, norm_first[...], norm_second[...], 0.25)
    total_out[...] = jnp.broadcast_to(total, total_out.shape)
    norm_clip_out[...] = clipped
    norm_first_out[...] = low
    norm_second_out[...] = high
    norm_params_out[...] = weight

    @pl.loop(0, capacity)
    def _(place):
        for number in range(len(outs)):
            send(number, place).wait()

    for move in moves:
        move.wait()


def finish_step(
    counts, owned, master, first, second, grad_rows, out_rows, squares, norm_sum, norm_params,
    norm_first, norm_second,
):
    tiles = jax.ShapeDtypeStruct(master.shape, F32)
    rows = jax.ShapeDtypeStruct(grad_rows.shape, F32)
    norms = jax.ShapeDtypeStruct(norm_params.shape, F32)
    return pl.pallas_call(
        finish_kernel,
        name="finish_step",
        out_shape=[
            tiles, tiles, tiles, tiles, jax.ShapeDtypeStruct(master.shape, BF16), rows, rows,
            jax.ShapeDtypeStruct((1, 128), F32), norms, norms, norms, norms,
        ],
        in_specs=[smem_spec()] + [vmem_spec()] * 11,
        out_specs=[any_spec()] * 7 + [vmem_spec()] * 5,
        scratch_shapes=[pltpu.VMEM(master.shape, F32)] * 4
        + [pltpu.VMEM(master.shape, BF16)]
        + [pltpu.VMEM(grad_rows.shape, F32)] * 2
        + [pltpu.SemaphoreType.DMA((5 * master.shape[0] + 2,))],
        compiler_params=pltpu.CompilerParams(vmem_limit_bytes=44 * 2**20),
        cost_estimate=pl.CostEstimate(
            flops=0, bytes_accessed=40 * 2**20, transcendentals=0
        ),
    )(
        counts, owned, master, first, second, grad_rows, out_rows, squares, norm_sum, norm_params,
        norm_first, norm_second,
    )


def local_by_rows(
    residual_in,
    cotangent,
    segments,
    owners,
    master_tiles,
    first_tiles,
    second_tiles,
    norm_params,
    norm_first,
    norm_second,
):
    local_rows, positions, model_width = residual_in.shape
    seq_devices = lax.axis_size("seq")
    seq_index = lax.axis_index("seq")
    length = positions * seq_devices
    tile_total = owners.shape[0]
    capacity, _, tile_width = master_tiles.shape
    quarter = capacity // 4
    pairs = model_width // tile_width
    places = jnp.arange(tile_total, dtype=jnp.int32)
    before = (owners[None, :] == owners[:, None]) & (places[None, :] < places[:, None])
    ranks = jnp.sum(before.astype(jnp.int32), axis=1)
    core, depth_z, part_id = owners % 2, owners // 2, ranks // quarter
    major = jnp.where(core == 0, part_id % 2, part_id // 2)
    minor = jnp.where(core == 0, part_id // 2, part_id % 2)
    weight_table = core * 64 + depth_z * 16 + ranks
    grad_table = (ranks % quarter) * 32 + core * 16 + major * 8 + minor * 4 + depth_z
    seats = jnp.arange(seq_devices, dtype=jnp.int32)
    counts = jnp.sum((owners[None, :] == seats[:, None]).astype(jnp.int32), axis=1)
    tiles, hidden = gather_start(master_tiles, residual_in)
    hidden = hidden.reshape(length, model_width)
    later, tiles = lax.optimization_barrier((cotangent, tiles))
    upper = lax.all_to_all(later.astype(BF16), "seq", split_axis=0, concat_axis=0, tiled=True)
    upper = upper.reshape(length, model_width)
    doc_ids = lax.dynamic_slice_in_dim(segments, seq_index, 1, 0)
    doc_row = doc_ids
    begin = jnp.sum((doc_ids < doc_ids[0, ::QUERY, None]).astype(jnp.int32), axis=1) // QUERY
    end = jnp.sum((doc_ids <= doc_ids[0, QUERY - 1 :: QUERY, None]).astype(jnp.int32), axis=1)
    many = (end - begin * QUERY + BLOCK - 1) // BLOCK
    spans = jnp.stack([jnp.minimum(begin, (length - many * BLOCK) // QUERY), many])
    *saved, after = forward_layers(
        weight_table, spans, norm_params, doc_row, hidden, tiles, pairs
    )
    out_rows = lax.all_to_all(
        after.reshape(residual_in.shape), "seq", split_axis=0, concat_axis=0, tiled=True
    )
    lower, held, norm_part = backward_layers(
        weight_table, grad_table, spans, counts, norm_params, doc_row, upper, saved, tiles,
    )
    owned, grad_rows, norm_sum, squares = reduce_end(
        held, lower.reshape(residual_in.shape), norm_part
    )
    (
        clipped, new_first, new_second, new_weight, new_copies, input_grad, residual_out,
        total, norm_clip, new_norm_f, new_norm_s, new_norm,
    ) = finish_step(
        counts, owned, master_tiles, first_tiles, second_tiles, grad_rows, out_rows, squares,
        norm_sum, norm_params, norm_first, norm_second,
    )
    return (
        residual_out,
        input_grad,
        clipped,
        total[0, :1],
        new_first,
        new_second,
        new_weight,
        new_copies,
        norm_clip,
        new_norm_f,
        new_norm_s,
        new_norm,
    )


def local(residual_in, *others):
    whole_rows = residual_in.shape[0] == lax.axis_size("seq")
    step = local_by_rows if whole_rows else local_by_heads
    return step(residual_in, *others)


def solution(mesh):
    by_rows = P("rows", "seq", None)
    by_slots = P("seq", None, None)
    return jax.shard_map(
        local,
        mesh=mesh,
        in_specs=(
            by_rows, by_rows, P("rows", None), P(), by_slots, by_slots, by_slots, P(), P(), P(),
        ),
        out_specs=(
            by_rows, by_rows, by_slots, P(), by_slots, by_slots, by_slots, by_slots,
            P(), P(), P(), P(),
        ),
        check_vma=False,
    )
```

profile of v0, /device:TPU:0, one launch (start us, length us, event | category | flops | bytes accessed | tf_op | source)
XLA Modules:
  0.0 357.1 jit_solution(13575625541087193339)
XLA Ops:
  0.6 0.0 copy-start
  0.7 75.9 %gather_start.1 = (bf16[128,512,128]{2,1,0:T(8,128)(2,1)}, bf16[8,128,512]{2,1,0:T(8,128)(2,1)}) custom-call(f32[16,512,128]{2,1,0:T(8,128)} %master.3, f32[8,128,512]{2,1,0:T(8,128)} %residual.1), custom_call_target="tpu_custom_call" | custom-call | bytes 209715200 | tf_op jit(solution)/shard_map/gather_start/pallas_call | solution.py:1139
  76.6 0.0 copy-start.14
  76.6 1.1 convert_element_type.19
  77.7 3.6 all-to-all-start
  81.3 0.6 convert_reduce_fusion.3.counts
  81.9 0.2 convert_reduce_fusion
  82.1 0.0 copy-start.13
  82.1 0.1 slice.10
  82.2 0.1 slice.9
  82.3 0.2 convert_reduce_fusion.2
  82.6 0.6 pad_add_fusion.spans
  83.2 0.5 fusion.9
  83.7 0.6 add_add_fusion.table
  84.3 47.2 %forward_layers.1 = (f32[2,1024,512]{2,1,0:T(8,128)}, bf16[2,1024,512]{2,1,0:T(8,128)(2,1)}, bf16[2,12,1024,128]{3,2,1,0:T(8,128)(2,1)}, bf16[2,4,1024,128]{3,2,...) custom-call(s32[96]{0:T(128)} %add_add_fusion.table, ...), custom_call_target="tpu_custom_call" | custom-call | flops 13958643712 | bytes 41943040 | tf_op jit(solution)/shard_map/forward_layers/pallas_call | solution.py:588
  131.5 3.9 %all-to-all-start.1 = ((bf16[8,128,512]{2,1,0:T(8,128)(2,1)}), bf16[8,128,512]{2,1,0:T(8,128)(2,1)S(1)}, u32[]{:S(2)}, u32[]{:S(2)}) async-start(bf16[8,128,512]{2,1,0:T(8,128)(2,1)} %bitcast.33), calls=%async_computation.1 | async-start | bytes 2097152 | tf_op jit(solution)/shard_map/all_to_all | solution.py:1545
  135.4 92.7 %backward_layers.1 = (bf16[1024,512]{1,0:T(8,128)(2,1)}, bf16[128,512,128]{2,1,0:T(8,128)(2,1)}, f32[8,512]{1,0:T(8,128)}) custom-call(s32[96]{0:T(128)} %add_add_fusion.table, s32[96]{0:T(128)} %get-tuple-element.76.aims, s32[2,8]{1,0:T(2,128)} %pad_add_fusion.spans, s32[8]{0:T(128)} %convert_reduce_fusion.3.counts, f32[8,512]{1,0:T(8,128)} %norm_params.1, ...), custom_call_target="tpu_custom_call" | custom-call | flops 32212254720 | bytes 62914560 | tf_op jit(solution)/shard_map/backward_layers/pallas_call | solution.py:882
  228.1 1.2 copy-done.5
  229.4 0.7 copy-done.6
  230.1 109.6 %reduce_end.1 = (bf16[16,512,128]{2,1,0:T(8,128)(2,1)S(1)}, bf16[8,128,512]{2,1,0:T(8,128)(2,1)S(1)}, f32[8,512]{1,0:T(8,128)S(1)}, f32[8,128]{1,0:T(8,128)S(1)}) custom-call(bf16[128,512,128]{2,1,0:T(8,128)(2,1)} %get-tuple-element.54.held, bf16[8,128,512]{2,1,0:T(8,128)(2,1)S(1)} %bitcast.31, f32[8,512]{1,0:T(8,128)S(1)} %copy-done.6), custom_call_target="tpu_custom_call" | custom-call | bytes 314572800 | tf_op jit(solution)/shard_map/reduce_end/pallas_call | solution.py:1362
  339.7 1.0 copy-done.3
  340.7 2.2 copy-done.2
  342.9 1.2 copy-done.4
  344.1 12.8 %finish_step.1 = (f32[16,512,128]{2,1,0:T(8,128)}, f32[16,512,128]{2,1,0:T(8,128)}, f32[16,512,128]{2,1,0:T(8,128)}, f32[16,512,128]{2,1,0:T(8,128)}, bf16[16,51...) custom-call(s32[8]{0:T(128)S(1)} %copy-done.10, ...), custom_call_target="tpu_custom_call" | custom-call | bytes 41943040 | tf_op jit(solution)/shard_map/finish_step/pallas_call | solution.py:1478
  (26 shorter events, 0.1 us)
Async XLA Ops:
  0.6 81.5 %copy-start = (s32[8,1024]{1,0:T(8,128)S(1)}, s32[8,1024]{1,0:T(8,128)}, u32[]{:S(2)}) copy-start(s32[8,1024]{1,0:T(8,128)} %param.12) | copy-start | bytes 98308
  0.7 75.9 %copy-start.11 = (f32[8,128,512]{2,1,0:T(8,128)S(1)}, f32[8,128,512]{2,1,0:T(8,128)}, u32[]{:S(2)}) copy-start(f32[8,128,512]{2,1,0:T(8,128)} %param.11) | copy-start | bytes 6291460
  76.6 4.7 %copy-start.14 = (s32[96]{0:T(128)S(1)}, s32[96]{0:T(128)}, u32[]{:S(2)}) copy-start(s32[96]{0:T(128)} %param.13) | copy-start | bytes 1156
  77.7 53.8 %all-to-all-start = ((bf16[8,128,512]{2,1,0:T(8,128)(2,1)}), bf16[8,128,512]{2,1,0:T(8,128)(2,1)S(1)}, u32[]{:S(2)}, u32[]{:S(2)}) async-start(bf16[8,128,512]{2,1,0:T(8,128)(2,1)} %convert_element_type.19), calls=%async_computation | async-start | bytes 2097152 | tf_op jit(solution)/shard_map/all_to_all | solution.py:1534
  82.1 2.2 copy-start.13
  131.5 3.9 %copy-start.12 = (bf16[8,128,512]{2,1,0:T(8,128)(2,1)}, bf16[8,128,512]{2,1,0:T(8,128)(2,1)S(1)}, u32[]{:S(2)}) copy-start(bf16[8,128,512]{2,1,0:T(8,128)(2,1)S(1)} %all-to-all-done) | copy-start | bytes 3145732
  131.5 209.1 %all-to-all-start.1 = ((bf16[8,128,512]{2,1,0:T(8,128)(2,1)}), bf16[8,128,512]{2,1,0:T(8,128)(2,1)S(1)}, u32[]{:S(2)}, u32[]{:S(2)}) async-start(bf16[8,128,512]{2,1,0:T(8,128)(2,1)} %bitcast.33), calls=%async_computation.1 | async-start | bytes 2097152 | tf_op jit(solution)/shard_map/all_to_all | solution.py:1545
  228.1 1.2 copy-start.5
  229.4 0.7 copy-start.6
  230.1 110.6 %copy-start.7 = (f32[8,512]{1,0:T(8,128)S(1)}, f32[8,512]{1,0:T(8,128)}, u32[]{:S(2)}) copy-start(f32[8,512]{1,0:T(8,128)} %norm_params.1) | copy-start | bytes 49156
  230.1 110.6 %copy-start.8 = (f32[8,512]{1,0:T(8,128)S(1)}, f32[8,512]{1,0:T(8,128)}, u32[]{:S(2)}) copy-start(f32[8,512]{1,0:T(8,128)} %norm_first.1) | copy-start | bytes 49156
  230.1 110.6 %copy-start.9 = (f32[8,512]{1,0:T(8,128)S(1)}, f32[8,512]{1,0:T(8,128)}, u32[]{:S(2)}) copy-start(f32[8,512]{1,0:T(8,128)} %norm_second.1) | copy-start | bytes 49156
  230.1 110.6 %copy-start.10 = (s32[8]{0:T(128)S(1)}, s32[8]{0:T(128)}, u32[]{:S(2)}) copy-start(s32[8]{0:T(128)} %convert_reduce_fusion.3.counts) | copy-start | bytes 100
  339.7 1.0 copy-start.3
  340.7 2.2 copy-start.2
  342.9 1.2 copy-start.4
  344.1 12.8 %copy-start.1 = (s32[8,1024]{1,0:T(8,128)S(1)}, s32[8,1024]{1,0:T(8,128)}, u32[]{:S(2)}) copy-start(s32[8,1024]{1,0:T(8,128)} %param.12) | copy-start | bytes 98308
where the time goes:
time: 357 us
  Pallas kernels  338 us (95%)
  starting transfers between devices  7.43 us (2%)
  local copies, waits for them, and re-layouts  6.56 us (2%)
  other arithmetic  3.84 us (1%)
    pallas_call x1, Pallas kernels, reduce_end(): pl.pallas_call(reduce_kernel, name='reduce_end', out_shape=[jax.ShapeDtyp...  110 us
    pallas_call x1, Pallas kernels, backward_layers(): pl.pallas_call(backward_kernel, name='backward_layers', out_shape=[jax.Sh...  92.7 us
    pallas_call x1, Pallas kernels, gather_start(): pl.pallas_call(gather_kernel, name='gather_start', out_shape=[jax.ShapeDt...  75.9 us
    pallas_call x1, Pallas kernels, forward_layers(): pl.pallas_call(forward_kernel, name='forward_layers', out_shape=[jax.Shap...  47.2 us
    pallas_call x1, Pallas kernels, finish_step(): pl.pallas_call(finish_kernel, name='finish_step', out_shape=[tiles, tiles...  12.8 us
  transfers between devices with their start and end apart: 2, of which 0 were waited for; matrix products, arithmetic and copies ran while one was open for 1% of the time, Pallas kernels for 70%

commit v1 on v0

--- a/solution.py
+++ b/solution.py
@@ -436,9 +436,9 @@
         again(1)
         fetch(layer, 0, "wait")
 
-        @pl.loop(0, blocks)
+        @pl.loop(0, length // 512)
         def _(number):
-            here = rows_of(number, DENSE)
+            here = rows_of(number, 512)
             unit, _ = normalized(flow[here, :])
             low = (unit * norms[pl.ds(4 * layer + 0, 1), :] + norms[pl.ds(4 * layer + 1, 1), :]).astype(BF16)
             normed[here, :] = low
@@ -514,9 +514,9 @@
         flush(6, layer).wait()
         chunk = width
 
-        @pl.loop(0, blocks)
+        @pl.loop(0, length // 1024)
         def _(number):
-            here = rows_of(number, DENSE)
+            here = rows_of(number, 1024)
             side_by_side = jnp.concatenate([mixed[pair, here, :] for pair in range(pairs)], axis=1)
             mid = flow[here, :] + dot_nn(side_by_side, w_out[layer])
             middle[here, :] = mid
@@ -684,7 +684,7 @@
     head_dim = width // HEADS
     own_head = 2 * lax.div(which, 8) + lax.rem(which, 8)
     fits = (lax.rem(which, 8) < 2) & (lax.div(lane, head_dim) == own_head)
-    selector[...] = jnp.where(fits, 1.0, 0.0)
+    selector[...] = jnp.where(fits, 1.0, 0.0).astype(BF16)
     take.wait()
     flow[...] = grad_low[...].astype(F32)
     chunk = 2 * width
@@ -751,7 +751,9 @@
                 mixed_grad[pair, here, :] = back[:, pair * lanes : (pair + 1) * lanes]
             side_by_side = jnp.concatenate([mixed[pair, here, :] for pair in range(pairs)], axis=1)
             both = side_by_side.astype(F32) * back.astype(F32)
-            sums = dot_nt(selector[...], both, precision=lax.Precision.HIGHEST)
+            high = both.astype(BF16)
+            rest = (both - high.astype(F32)).astype(BF16)
+            sums = dot_nt(selector[...], high) + dot_nt(selector[...], rest)
             for pair in range(pairs):
                 delta[pair, :, here] = sums[8 * pair : 8 * pair + 8, :]
 
@@ -915,7 +917,7 @@
             pltpu.VMEM((48, width, lanes), BF16),
             pltpu.VMEM((width, lanes), BF16),
             pltpu.VMEM((length, lanes), jnp.int32),
-            pltpu.VMEM((8 * pairs, width), F32),
+            pltpu.VMEM((8 * pairs, width), BF16),
             pltpu.SemaphoreType.DMA((48 * LAYERS,)),
             pltpu.SemaphoreType.DMA((7,)),
             pltpu.SemaphoreType.DMA((48,)),
@@ -1015,15 +1017,15 @@
         return make(tiles.at[part], tiles.at[part], number, partner)
 
     mine = pl.ds(core * 64 + z * 16, 16)
-    own_here = pl.ds(spot(z, quarter_id), 4)
-
-    def hop(way, step):
+
+    def hop(way, step, half):
         toward = device_at(x, y, lax.rem(z + (1 if way == 0 else 3), 4), core)
-        number = 3 * way + step - 1
+        number = 6 * way + 2 * (step - 1) + half
         if step == 1:
-            return make(low.at[pl.ds(4 * quarter_id, 4)], tiles.at[own_here], number, toward)
+            near = pl.ds(spot(z, quarter_id) + 2 * half, 2)
+            return make(low.at[pl.ds(4 * quarter_id + 2 * half, 2)], tiles.at[near], number, toward)
         z_from = lax.rem(z + (5 - step if way == 0 else step - 1), 4)
-        return relay(number, spot(z_from, quarter_id), 4, toward)
+        return relay(number, spot(z_from, quarter_id) + 2 * half, 2, toward)
 
     def can_send(way, step):
         if way == 0:
@@ -1036,33 +1038,35 @@
     def source(way, step):
         return lax.rem(z + (4 - step if way == 0 else step), 4)
 
-    steps = [(way, step) for step in range(1, 4) for way in range(2)]
-
-    def fan(way, step):
-        base = 6 + 9 * (3 * way + step - 1)
+    rounds = [
+        [(way, step, half) for half in range(2) for way in range(2)] for step in range(1, 4)
+    ]
+    steps = rounds[0] + rounds[1] + rounds[2]
+
+    def fan(way, step, half):
+        base = 12 + 7 * (6 * way + 2 * (step - 1) + half)
         z_from = source(way, step)
+        spots = [spot(z_from, quarter) + 2 * half for quarter in quarters]
         return [
-            relay(base, spot(z_from, quarters[0]), 4, by_x),
-            relay(base + 1, spot(z_from, quarters[0]), 4, by_y),
-            relay(base + 2, spot(z_from, quarters[0]), 4, across),
-            relay(base + 3, spot(z_from, quarters[1]), 2, by_y),
-            relay(base + 4, spot(z_from, quarters[1]), 4, across),
-            relay(base + 5, spot(z_from, quarters[2]) + 2, 2, by_x),
-            relay(base + 6, spot(z_from, quarters[2]), 4, across),
-            relay(base + 7, spot(z_from, quarters[3]), 2, across),
-            relay(base + 8, spot(z_from, quarters[3]) + 2, 2, across),
+            relay(base, spots[0], 2, by_x),
+            relay(base + 1, spots[0], 2, by_y),
+            relay(base + 2, spots[0], 2, across),
+            relay(base + 3, spots[1 + half], 2, by_x if half else by_y),
+            relay(base + 4, spots[1], 2, across),
+            relay(base + 5, spots[2], 2, across),
+            relay(base + 6, spots[3], 2, across),
         ]
 
     load_near.wait()
     convert(4 * quarter_id, 4)
-    for way in range(2):
-        pl.when(can_send(way, 1))(lambda way=way: hop(way, 1).start())
+    for way, step, half in rounds[0]:
+        pl.when(can_send(way, 1))(lambda way=way, half=half: hop(way, 1, half).start())
     for k in range(1, 4):
         far[k - 1].wait()
         convert(4 * ((quarter_id + k) % 4), 4)
     keep_tiles = pltpu.make_async_copy(low, tiles.at[mine], l_sem.at[6])
     keep_tiles.start()
-    own_across = make(low, tiles.at[mine], 60, across)
+    own_across = make(low, tiles.at[mine], 96, across)
     own_across.start()
     load_flat.wait()
 
@@ -1073,58 +1077,59 @@
     keep_row = pltpu.make_async_copy(flat_low.at[seat], rows.at[seat], l_sem.at[5])
     keep_row.start()
     row_moves = [
-        make(flat_low.at[(seat + k) % 8], rows.at[seat], 60 + k, seats[k - 1])
+        make(flat_low.at[(seat + k) % 8], rows.at[seat], 96 + k, seats[k - 1])
         for k in range(1, 8)
     ]
 
-    def take(way, step):
-        hop(way, step).wait_recv()
+    def take(way, step, half):
+        hop(way, step, half).wait_recv()
         if step < 3:
-            pl.when(can_send(way, step + 1))(lambda: hop(way, step + 1).start())
-        for copy in fan(way, step)[:3]:
+            pl.when(can_send(way, step + 1))(lambda: hop(way, step + 1, half).start())
+        for copy in fan(way, step, half)[:3]:
             copy.start()
 
-    def turn(way, step):
-        moves = fan(way, step)
-        moves[0].wait_recv()
-        moves[3].start()
-        moves[4].start()
-        moves[1].wait_recv()
-        moves[5].start()
+    def turn(way, step, half):
+        moves = fan(way, step, half)
+        for side in (half, 1 - half):
+            moves[side].wait_recv()
+            if side == half:
+                moves[3].start()
+            moves[4 + side].start()
+
+    def finish(way, step, half):
+        moves = fan(way, step, half)
+        moves[3].wait_recv()
         moves[6].start()
 
-    def finish(way, step):
-        moves = fan(way, step)
-        moves[3].wait_recv()
-        moves[7].start()
-        moves[5].wait_recv()
-        moves[8].start()
-
-    def drain(way, step):
-        moves = fan(way, step)
-        for number in (2, 4, 6, 7, 8):
+    def drain(way, step, half):
+        moves = fan(way, step, half)
+        for number in (2, 4, 5, 6):
             moves[number].wait_recv()
         for copy in moves:
             copy.wait_send()
 
     def each(act, chosen):
-        for way, step in chosen:
-            pl.when(arrives(way, step))(lambda way=way, step=step: act(way, step))
-
-    each(take, steps[:2])
-    each(take, steps[2:4])
-    each(turn, steps[:2])
-    each(take, steps[4:])
+        for key in chosen:
+            pl.when(arrives(key[0], key[1]))(lambda key=key: act(*key))
+
+    each(take, rounds[0])
+    each(take, rounds[1][:2])
+    each(turn, rounds[0][:2])
+    each(take, rounds[1][2:])
+    each(turn, rounds[0][2:])
+    each(take, rounds[2])
     for copy in row_moves:
         copy.start()
-    each(turn, steps[2:4])
-    each(finish, steps[:2])
-    each(turn, steps[4:])
-    each(finish, steps[2:])
+    each(turn, rounds[1])
+    each(finish, rounds[0])
+    each(turn, rounds[2])
+    each(finish, rounds[1] + rounds[2])
     own_across.wait_recv()
     each(drain, steps)
-    for way, step in steps:
-        pl.when(can_send(way, step))(lambda way=way, step=step: hop(way, step).wait_send())
+    for way, step, half in steps:
+        pl.when(can_send(way, step))(
+            lambda way=way, step=step, half=half: hop(way, step, half).wait_send()
+        )
     for copy in row_moves:
         copy.wait_recv()
         copy.wait_send()
@@ -1135,7 +1140,7 @@
 
 def gather_start(master_tiles, residual):
     capacity, depth, lanes = master_tiles.shape
-    count = 68
+    count = 104
     return pl.pallas_call(
         gather_kernel,
         name="gather_start",
@@ -1386,7 +1391,7 @@
             pltpu.SemaphoreType.DMA((3 * chunks + 1,)),
         ],
         compiler_params=pltpu.CompilerParams(
-            collective_id=1, has_side_effects=True, vmem_limit_bytes=40 * 2**20
+            collective_id=1, has_side_effects=True, vmem_limit_bytes=VMEM_BYTES
         ),
         cost_estimate=pl.CostEstimate(
             flops=0, bytes_accessed=300 * 2**20, transcendentals=0
@@ -1395,12 +1400,35 @@
 
 
 def finish_kernel(
-    counts, owned, master, first, second, grad_rows, out_rows, squares, norm_sum, norm_params,
-    norm_first, norm_second,
+    counts, owned_in, master_in, first_in, second_in, grad_rows_in, out_rows_in, squares, norm_sum,
+    norm_params, norm_first, norm_second,
     clip_out, first_out, second_out, master_out, copy_out, grad_rows_out, out_rows_out,
     total_out, norm_clip_out, norm_first_out, norm_second_out, norm_params_out,
-    clip, new_first, new_second, new_master, new_copy, wide_grad, wide_out, o_sem,
+    owned, master, first, second, grad_rows, out_rows,
+    clip, new_first, new_second, new_master, new_copy, wide_grad, wide_out, i_sem, o_sem,
 ):
+    ins = ((owned_in, owned), (master_in, master), (first_in, first), (second_in, second))
+    capacity = master.shape[0]
+
+    def bring(number, place):
+        return pltpu.make_async_copy(
+            ins[number][0].at[place], ins[number][1].at[place],
+            i_sem.at[number * capacity + place],
+        )
+
+    @pl.loop(0, capacity)
+    def _(place):
+        for number in range(len(ins)):
+            bring(number, place).start()
+
+    bring_rows = [
+        pltpu.make_async_copy(source, target, i_sem.at[4 * capacity + number])
+        for number, (source, target) in enumerate(
+            ((grad_rows_in, grad_rows), (out_rows_in, out_rows))
+        )
+    ]
+    for copy in bring_rows:
+        copy.start()
     norms = norm_sum[...]
     total = jnp.sqrt(jnp.sum(squares[...]) + jnp.sum(norms * norms))
     factor = 1.0 / jnp.maximum(total, 1.0)
@@ -1416,7 +1444,6 @@
         (clip, clip_out), (new_first, first_out), (new_second, second_out),
         (new_master, master_out), (new_copy, copy_out),
     )
-    capacity = master.shape[0]
 
     def send(number, place):
         return pltpu.make_async_copy(
@@ -1428,6 +1455,8 @@
 
     @pl.loop(0, capacity)
     def _(place):
+        for number in range(len(ins)):
+            bring(number, place).wait()
         keep = (lax.broadcast(place, clip.shape[1:])) < count
         grad = jnp.where(keep, owned[place].astype(F32), 0.0) * factor
         weight, low, high = step(master[place], grad, first[place], second[place], 0.05)
@@ -1444,6 +1473,8 @@
     for number, (low, wide, target) in enumerate(
         ((grad_rows, wide_grad, grad_rows_out), (out_rows, wide_out, out_rows_out))
     ):
+
+        bring_rows[number].wait()
 
         @pl.loop(0, low.shape[0])
         def _(j, low=low, wide=wide):
@@ -1482,13 +1513,17 @@
             tiles, tiles, tiles, tiles, jax.ShapeDtypeStruct(master.shape, BF16), rows, rows,
             jax.ShapeDtypeStruct((1, 128), F32), norms, norms, norms, norms,
         ],
-        in_specs=[smem_spec()] + [vmem_spec()] * 11,
+        in_specs=[smem_spec()] + [any_spec()] * 6 + [vmem_spec()] * 5,
         out_specs=[any_spec()] * 7 + [vmem_spec()] * 5,
-        scratch_shapes=[pltpu.VMEM(master.shape, F32)] * 4
+        scratch_shapes=[pltpu.VMEM(owned.shape, BF16)]
+        + [pltpu.VMEM(master.shape, F32)] * 3
+        + [pltpu.VMEM(grad_rows.shape, BF16)] * 2
+        + [pltpu.VMEM(master.shape, F32)] * 4
         + [pltpu.VMEM(master.shape, BF16)]
         + [pltpu.VMEM(grad_rows.shape, F32)] * 2
+        + [pltpu.SemaphoreType.DMA((4 * master.shape[0] + 2,))]
         + [pltpu.SemaphoreType.DMA((5 * master.shape[0] + 2,))],
-        compiler_params=pltpu.CompilerParams(vmem_limit_bytes=44 * 2**20),
+        compiler_params=pltpu.CompilerParams(vmem_limit_bytes=VMEM_BYTES),
         cost_estimate=pl.CostEstimate(
             flops=0, bytes_accessed=40 * 2**20, transcendentals=0
         ),

time: 357 us -> 348 us (0.975)
  Pallas kernels: 338 us -> 332 us
  local copies, waits for them, and re-layouts: 6.56 us -> 1.2 us
    unnamed x30 -> x14, local copies, waits for them, and re-layouts: 6.36 us -> 1 us
    pallas_call x1, Pallas kernels: 92.7 us -> 87.5 us  [backward_layers(): pl.pallas_call(backward_kernel, name='backward_layers', out_shape=[jax.Sh...]
    pallas_call x1, Pallas kernels: 75.9 us -> 71.4 us  [gather_start(): pl.pallas_call(gather_kernel, name='gather_start', out_shape=[jax.ShapeDt...]
    pallas_call x1, Pallas kernels: 47.2 us -> 43.3 us  [forward_layers(): pl.pallas_call(forward_kernel, name='forward_layers', out_shape=[jax.Shap...]
    pallas_call x1, Pallas kernels: 110 us -> 113 us  [reduce_end(): pl.pallas_call(reduce_kernel, name='reduce_end', out_shape=[jax.ShapeDtyp...]
    pallas_call x1, Pallas kernels: 12.8 us -> 16.4 us  [finish_step(): pl.pallas_call(finish_kernel, name='finish_step', out_shape=[tiles, tiles...]
where the time goes in v1:
time: 348 us; the launch traced here: 347 us
  Pallas kernels  332 us (95%)
  starting transfers between devices  9.26 us (3%)
  other arithmetic  3.86 us (1%)
    pallas_call x1, Pallas kernels, reduce_end(): pl.pallas_call(reduce_kernel, name='reduce_end', out_shape=[jax.ShapeDtyp...  113 us
    pallas_call x1, Pallas kernels, backward_layers(): pl.pallas_call(backward_kernel, name='backward_layers', out_shape=[jax.Sh...  87.5 us
    pallas_call x1, Pallas kernels, gather_start(): pl.pallas_call(gather_kernel, name='gather_start', out_shape=[jax.ShapeDt...  71.4 us
    pallas_call x1, Pallas kernels, forward_layers(): pl.pallas_call(forward_kernel, name='forward_layers', out_shape=[jax.Shap...  43.3 us
    pallas_call x1, Pallas kernels, finish_step(): pl.pallas_call(finish_kernel, name='finish_step', out_shape=[tiles, tiles...  16.4 us
  transfers between devices with their start and end apart: 2, of which 0 were waited for; matrix products, arithmetic and copies ran while one was open for 1% of the time, Pallas kernels for 70%

profile of v1, /device:TPU:0, one launch (start us, length us, event | category | flops | bytes accessed | tf_op | source)
XLA Modules:
  0.0 347.4 jit_solution(1569192152998324884)
XLA Ops:
  0.6 0.0 copy-start
  0.7 0.0 copy-start.3
  0.7 71.4 %gather_start.1 = (bf16[128,512,128]{2,1,0:T(8,128)(2,1)}, bf16[8,128,512]{2,1,0:T(8,128)(2,1)}) custom-call(f32[16,512,128]{2,1,0:T(8,128)} %master_in.1, f32[8,128,512]{2,1,0:T(8,128)} %residual.1), custom_call_target="tpu_custom_call" | custom-call | bytes 209715200 | tf_op jit(solution)/shard_map/gather_start/pallas_call | solution.py:1144
  72.1 0.0 copy-start.6
  72.1 1.1 convert_element_type.19
  73.2 3.6 %all-to-all-start = ((bf16[8,128,512]{2,1,0:T(8,128)(2,1)}), bf16[8,128,512]{2,1,0:T(8,128)(2,1)S(1)}, u32[]{:S(2)}, u32[]{:S(2)}) async-start(bf16[8,128,512]{2,1,0:T(8,128)(2,1)} %convert_element_type.19), calls=%async_computation | async-start | bytes 2097152 | tf_op jit(solution)/shard_map/all_to_all | solution.py:1569
  76.8 0.7 convert_reduce_fusion.3.counts
  77.5 0.2 convert_reduce_fusion
  77.7 0.0 copy-start.5
  77.7 0.1 slice.10
  77.8 0.1 slice.9
  77.9 0.2 convert_reduce_fusion.2
  78.2 0.6 pad_add_fusion.spans
  78.8 0.5 fusion.9
  79.3 0.5 add_add_fusion.table
  79.8 43.3 %forward_layers.1 = (f32[2,1024,512]{2,1,0:T(8,128)}, bf16[2,1024,512]{2,1,0:T(8,128)(2,1)}, bf16[2,12,1024,128]{3,2,1,0:T(8,128)(2,1)}, bf16[2,4,1024,128]{3,2,...) custom-call(s32[96]{0:T(128)} %add_add_fusion.table, ...), custom_call_target="tpu_custom_call" | custom-call | flops 13958643712 | bytes 41943040 | tf_op jit(solution)/shard_map/forward_layers/pallas_call | solution.py:588
  123.1 0.0 all-to-all-done
  123.1 0.0 copy-start.4
  123.1 5.7 %all-to-all-start.1 = ((bf16[8,128,512]{2,1,0:T(8,128)(2,1)}), bf16[8,128,512]{2,1,0:T(8,128)(2,1)S(1)}, u32[]{:S(2)}, u32[]{:S(2)}) async-start(bf16[8,128,512]{2,1,0:T(8,128)(2,1)} %bitcast.33), calls=%async_computation.1 | async-start | bytes 2097152 | tf_op jit(solution)/shard_map/all_to_all | solution.py:1580
  128.8 87.5 %backward_layers.1 = (bf16[1024,512]{1,0:T(8,128)(2,1)}, bf16[128,512,128]{2,1,0:T(8,128)(2,1)}, f32[8,512]{1,0:T(8,128)}) custom-call(s32[96]{0:T(128)} %add_add_fusion.table, s32[96]{0:T(128)} %get-tuple-element.76.aims, s32[2,8]{1,0:T(2,128)} %pad_add_fusion.spans, s32[8]{0:T(128)} %convert_reduce_fusion.3.counts, f32[8,512]{1,0:T(8,128)} %norm_params.1, ...), custom_call_target="tpu_custom_call" | custom-call | flops 32212254720 | bytes 62914560 | tf_op jit(solution)/shard_map/backward_layers/pallas_call | solution.py:884
  216.4 113.4 %reduce_end.1 = (bf16[16,512,128]{2,1,0:T(8,128)(2,1)}, bf16[8,128,512]{2,1,0:T(8,128)(2,1)}, f32[8,512]{1,0:T(8,128)}, f32[8,128]{1,0:T(8,128)}) custom-call(bf16[128,512,128]{2,1,0:T(8,128)(2,1)} %get-tuple-element.54.held, bf16[8,128,512]{2,1,0:T(8,128)(2,1)} %bitcast.31, f32[8,512]{1,0:T(8,128)} %get-tuple-element.56.norm_part), custom_call_target="tpu_custom_call" | custom-call | bytes 314572800 | tf_op jit(solution)/shard_map/reduce_end/pallas_call | solution.py:1367
  329.8 0.0 all-to-all-done.1.out_rows_in
  329.8 1.0 copy-done.2
  330.8 16.4 %finish_step.1 = (f32[16,512,128]{2,1,0:T(8,128)}, f32[16,512,128]{2,1,0:T(8,128)}, f32[16,512,128]{2,1,0:T(8,128)}, f32[16,512,128]{2,1,0:T(8,128)}, bf16[16,51...) custom-call(s32[8]{0:T(128)} %convert_reduce_fusion.3.counts, ...), custom_call_target="tpu_custom_call" | custom-call | bytes 41943040 | tf_op jit(solution)/shard_map/finish_step/pallas_call | solution.py:1509
  (10 shorter events, 0.1 us)
Async XLA Ops:
  0.6 77.0 %copy-start = (s32[8,1024]{1,0:T(8,128)S(1)}, s32[8,1024]{1,0:T(8,128)}, u32[]{:S(2)}) copy-start(s32[8,1024]{1,0:T(8,128)} %param.12) | copy-start | bytes 98308
  0.7 71.4 %copy-start.3 = (f32[8,128,512]{2,1,0:T(8,128)S(1)}, f32[8,128,512]{2,1,0:T(8,128)}, u32[]{:S(2)}) copy-start(f32[8,128,512]{2,1,0:T(8,128)} %param.11) | copy-start | bytes 6291460
  72.1 4.7 %copy-start.6 = (s32[96]{0:T(128)S(1)}, s32[96]{0:T(128)}, u32[]{:S(2)}) copy-start(s32[96]{0:T(128)} %param.13) | copy-start | bytes 1156
  73.2 49.9 %all-to-all-start = ((bf16[8,128,512]{2,1,0:T(8,128)(2,1)}), bf16[8,128,512]{2,1,0:T(8,128)(2,1)S(1)}, u32[]{:S(2)}, u32[]{:S(2)}) async-start(bf16[8,128,512]{2,1,0:T(8,128)(2,1)} %convert_element_type.19), calls=%async_computation | async-start | bytes 2097152 | tf_op jit(solution)/shard_map/all_to_all | solution.py:1569
  77.7 2.1 copy-start.5
  123.1 5.7 %copy-start.4 = (bf16[8,128,512]{2,1,0:T(8,128)(2,1)}, bf16[8,128,512]{2,1,0:T(8,128)(2,1)S(1)}, u32[]{:S(2)}) copy-start(bf16[8,128,512]{2,1,0:T(8,128)(2,1)S(1)} %all-to-all-done) | copy-start | bytes 3145732
  123.1 206.7 %all-to-all-start.1 = ((bf16[8,128,512]{2,1,0:T(8,128)(2,1)}), bf16[8,128,512]{2,1,0:T(8,128)(2,1)S(1)}, u32[]{:S(2)}, u32[]{:S(2)}) async-start(bf16[8,128,512]{2,1,0:T(8,128)(2,1)} %bitcast.33), calls=%async_computation.1 | async-start | bytes 2097152 | tf_op jit(solution)/shard_map/all_to_all | solution.py:1580
  329.8 1.0 copy-start.2
  330.8 16.5 %copy-start.1 = (s32[8,1024]{1,0:T(8,128)S(1)}, s32[8,1024]{1,0:T(8,128)}, u32[]{:S(2)}) copy-start(s32[8,1024]{1,0:T(8,128)} %param.12) | copy-start | bytes 98308

commit v2 on v1

--- a/solution.py
+++ b/solution.py
@@ -955,11 +955,10 @@
 
 
 def seat_partners(x, y, z, core):
-    others = []
-    for k in range(1, 8):
-        seat = (2 * z + core + k) % 8
-        others.append((2 * y + x, seat))
-    return others
+    mirrored = (3 - z, (z + 2) % 4, z + 1 - 2 * (z % 2))
+    others = [2 * far + side for far in mirrored for side in (core, 1 - core)]
+    others.append(2 * z + 1 - core)
+    return others, [(2 * y + x, other) for other in others]
 
 
 def post(source, target, send_sem, recv_sem, number, partner):
@@ -982,7 +981,7 @@
     by_x = device_at(1 - x, y, z, core)
     by_y = device_at(x, 1 - y, z, core)
     quarters = (quarter_id, 2 * y + (1 - x), 2 * (1 - y) + x, 3 - quarter_id)
-    seats = seat_partners(x, y, z, core)
+    others, seats = seat_partners(x, y, z, core)
     seat = 2 * z + core
     load_near = pltpu.make_async_copy(
         master.at[pl.ds(4 * quarter_id, 4)], wide.at[pl.ds(4 * quarter_id, 4)], l_sem.at[0]
@@ -1077,7 +1076,7 @@
     keep_row = pltpu.make_async_copy(flat_low.at[seat], rows.at[seat], l_sem.at[5])
     keep_row.start()
     row_moves = [
-        make(flat_low.at[(seat + k) % 8], rows.at[seat], 96 + k, seats[k - 1])
+        make(flat_low.at[others[k - 1]], rows.at[seat], 96 + k, seats[k - 1])
         for k in range(1, 8)
     ]
 
@@ -1185,7 +1184,7 @@
     one = device_at(x + minus * (1 - 2 * x), y + plus * (1 - 2 * y), z, core)
     two = device_at(x + plus * (1 - 2 * x), y + minus * (1 - 2 * y), z, core)
     along_z = [device_at(x, y, (z + k) % 4, core) for k in range(1, 4)]
-    seats = seat_partners(x, y, z, core)
+    others, seats = seat_partners(x, y, z, core)
     seat = 2 * z + core
     quarter_x, quarter_y = 2 * y + (1 - x), 2 * (1 - y) + x
     chunks = own.shape[0]
@@ -1216,7 +1215,7 @@
     norm_now[0] = norm_part[...]
     norm_moves = [move(norm_now.at[0], norm_in.at[0], across)]
     for k in range(1, 8):
-        move(upper.at[(seat + k) % 8], rows.at[seat], seats[k - 1])
+        move(upper.at[others[k - 1]], rows.at[seat], seats[k - 1])
     row_moves = copies[-7:]
     keep_row = pltpu.make_async_copy(upper.at[seat], rows.at[seat], l_sem.at[chunks])
     keep_row.start()

time: 348 us -> 348 us (level)
  no operation moved by 1% of the time
where the time goes in v2:
time: 348 us; the launch traced here: 347 us
  Pallas kernels  330 us (95%)
  starting transfers between devices  10.6 us (3%)
  other arithmetic  3.86 us (1%)
    pallas_call x1, Pallas kernels, reduce_end(): pl.pallas_call(reduce_kernel, name='reduce_end', out_shape=[jax.ShapeDtyp...  112 us
    pallas_call x1, Pallas kernels, backward_layers(): pl.pallas_call(backward_kernel, name='backward_layers', out_shape=[jax.Sh...  88.9 us
    pallas_call x1, Pallas kernels, gather_start(): pl.pallas_call(gather_kernel, name='gather_start', out_shape=[jax.ShapeDt...  69.3 us
    pallas_call x1, Pallas kernels, forward_layers(): pl.pallas_call(forward_kernel, name='forward_layers', out_shape=[jax.Shap...  44 us
    pallas_call x1, Pallas kernels, finish_step(): pl.pallas_call(finish_kernel, name='finish_step', out_shape=[tiles, tiles...  16.4 us
  transfers between devices with their start and end apart: 2, of which 0 were waited for; matrix products, arithmetic and copies ran while one was open for 1% of the time, Pallas kernels for 70%

profile of v2, /device:TPU:0, one launch (start us, length us, event | category | flops | bytes accessed | tf_op | source)
XLA Modules:
  0.0 346.9 jit_solution(4306049502145698938)
XLA Ops:
  0.6 0.0 copy-start
  0.7 69.3 %gather_start.1 = (bf16[128,512,128]{2,1,0:T(8,128)(2,1)}, bf16[8,128,512]{2,1,0:T(8,128)(2,1)}) custom-call(f32[16,512,128]{2,1,0:T(8,128)} %master_in.1, f32[8,128,512]{2,1,0:T(8,128)} %residual.1), custom_call_target="tpu_custom_call" | custom-call | bytes 209715200 | tf_op jit(solution)/shard_map/gather_start/pallas_call | solution.py:1143
  69.9 0.0 copy-start.6
  70.0 0.0 copy-done.3
  70.0 1.1 convert_element_type.19
  71.1 4.5 %all-to-all-start = ((bf16[8,128,512]{2,1,0:T(8,128)(2,1)}), bf16[8,128,512]{2,1,0:T(8,128)(2,1)S(1)}, u32[]{:S(2)}, u32[]{:S(2)}) async-start(bf16[8,128,512]{2,1,0:T(8,128)(2,1)} %convert_element_type.19), calls=%async_computation | async-start | bytes 2097152 | tf_op jit(solution)/shard_map/all_to_all | solution.py:1568
  75.6 0.7 convert_reduce_fusion.3.counts
  76.3 0.2 convert_reduce_fusion
  76.5 0.0 copy-start.5
  76.5 0.1 slice.10
  76.6 0.1 slice.9
  76.7 0.2 convert_reduce_fusion.2
  77.0 0.6 pad_add_fusion.spans
  77.6 0.5 fusion.9
  78.1 0.5 add_add_fusion.table
  78.6 44.0 %forward_layers.1 = (f32[2,1024,512]{2,1,0:T(8,128)}, bf16[2,1024,512]{2,1,0:T(8,128)(2,1)}, bf16[2,12,1024,128]{3,2,1,0:T(8,128)(2,1)}, bf16[2,4,1024,128]{3,2,...) custom-call(s32[96]{0:T(128)} %add_add_fusion.table, ...), custom_call_target="tpu_custom_call" | custom-call | flops 13958643712 | bytes 41943040 | tf_op jit(solution)/shard_map/forward_layers/pallas_call | solution.py:588
  122.6 0.0 all-to-all-done
  122.6 0.0 copy-start.4
  122.6 6.0 %all-to-all-start.1 = ((bf16[8,128,512]{2,1,0:T(8,128)(2,1)}), bf16[8,128,512]{2,1,0:T(8,128)(2,1)S(1)}, u32[]{:S(2)}, u32[]{:S(2)}) async-start(bf16[8,128,512]{2,1,0:T(8,128)(2,1)} %bitcast.33), calls=%async_computation.1 | async-start | bytes 2097152 | tf_op jit(solution)/shard_map/all_to_all | solution.py:1579
  128.7 88.9 %backward_layers.1 = (bf16[1024,512]{1,0:T(8,128)(2,1)}, bf16[128,512,128]{2,1,0:T(8,128)(2,1)}, f32[8,512]{1,0:T(8,128)}) custom-call(s32[96]{0:T(128)} %add_add_fusion.table, s32[96]{0:T(128)} %get-tuple-element.76.aims, s32[2,8]{1,0:T(2,128)} %pad_add_fusion.spans, s32[8]{0:T(128)} %convert_reduce_fusion.3.counts, f32[8,512]{1,0:T(8,128)} %norm_params.1, ...), custom_call_target="tpu_custom_call" | custom-call | flops 32212254720 | bytes 62914560 | tf_op jit(solution)/shard_map/backward_layers/pallas_call | solution.py:884
  217.6 111.6 %reduce_end.1 = (bf16[16,512,128]{2,1,0:T(8,128)(2,1)}, bf16[8,128,512]{2,1,0:T(8,128)(2,1)}, f32[8,512]{1,0:T(8,128)}, f32[8,128]{1,0:T(8,128)}) custom-call(bf16[128,512,128]{2,1,0:T(8,128)(2,1)} %get-tuple-element.54.held, bf16[8,128,512]{2,1,0:T(8,128)(2,1)} %bitcast.31, f32[8,512]{1,0:T(8,128)} %get-tuple-element.56.norm_part), custom_call_target="tpu_custom_call" | custom-call | bytes 314572800 | tf_op jit(solution)/shard_map/reduce_end/pallas_call | solution.py:1366
  329.2 0.0 all-to-all-done.1.out_rows_in
  329.3 1.0 copy-done.2
  330.2 16.4 %finish_step.1 = (f32[16,512,128]{2,1,0:T(8,128)}, f32[16,512,128]{2,1,0:T(8,128)}, f32[16,512,128]{2,1,0:T(8,128)}, f32[16,512,128]{2,1,0:T(8,128)}, bf16[16,51...) custom-call(s32[8]{0:T(128)} %convert_reduce_fusion.3.counts, ...), custom_call_target="tpu_custom_call" | custom-call | bytes 41943040 | tf_op jit(solution)/shard_map/finish_step/pallas_call | solution.py:1508
  (10 shorter events, 0.1 us)
Async XLA Ops:
  0.6 75.9 %copy-start = (s32[8,1024]{1,0:T(8,128)S(1)}, s32[8,1024]{1,0:T(8,128)}, u32[]{:S(2)}) copy-start(s32[8,1024]{1,0:T(8,128)} %param.12) | copy-start | bytes 98308
  0.7 69.3 %copy-start.3 = (f32[8,128,512]{2,1,0:T(8,128)S(1)}, f32[8,128,512]{2,1,0:T(8,128)}, u32[]{:S(2)}) copy-start(f32[8,128,512]{2,1,0:T(8,128)} %param.11) | copy-start | bytes 6291460
  69.9 5.7 %copy-start.6 = (s32[96]{0:T(128)S(1)}, s32[96]{0:T(128)}, u32[]{:S(2)}) copy-start(s32[96]{0:T(128)} %param.13) | copy-start | bytes 1156
  71.1 51.5 %all-to-all-start = ((bf16[8,128,512]{2,1,0:T(8,128)(2,1)}), bf16[8,128,512]{2,1,0:T(8,128)(2,1)S(1)}, u32[]{:S(2)}, u32[]{:S(2)}) async-start(bf16[8,128,512]{2,1,0:T(8,128)(2,1)} %convert_element_type.19), calls=%async_computation | async-start | bytes 2097152 | tf_op jit(solution)/shard_map/all_to_all | solution.py:1568
  76.5 2.1 copy-start.5
  122.6 6.0 %copy-start.4 = (bf16[8,128,512]{2,1,0:T(8,128)(2,1)}, bf16[8,128,512]{2,1,0:T(8,128)(2,1)S(1)}, u32[]{:S(2)}) copy-start(bf16[8,128,512]{2,1,0:T(8,128)(2,1)S(1)} %all-to-all-done) | copy-start | bytes 3145732
  122.6 206.6 %all-to-all-start.1 = ((bf16[8,128,512]{2,1,0:T(8,128)(2,1)}), bf16[8,128,512]{2,1,0:T(8,128)(2,1)S(1)}, u32[]{:S(2)}, u32[]{:S(2)}) async-start(bf16[8,128,512]{2,1,0:T(8,128)(2,1)} %bitcast.33), calls=%async_computation.1 | async-start | bytes 2097152 | tf_op jit(solution)/shard_map/all_to_all | solution.py:1579
  329.3 1.0 copy-start.2
  330.2 16.5 %copy-start.1 = (s32[8,1024]{1,0:T(8,128)S(1)}, s32[8,1024]{1,0:T(8,128)}, u32[]{:S(2)}) copy-start(s32[8,1024]{1,0:T(8,128)} %param.12) | copy-start | bytes 98308
